TPU v7x, 32 devices: a whole 2x2x4 slice. The times are simulated.
32 devices in a mesh: dp: 8 (over y, x, core), mp: 4 (over z).
Axes of the slice: x: 2, y: 2, z: 4, core: 2. Of those that a mesh axis runs over, the one named last changes fastest.
Arguments:
- frames_long: bfloat16 [8, 1024, 768], P('dp', 'mp'), may hold values from -6 to 6
- frames_short: bfloat16 [16, 512, 768], P('dp', 'mp'), may hold values from -6 to 6
- length_long: int32 [8], P('dp'), may hold values from 513 to 1024, as said below
- length_short: int32 [16], P('dp'), may hold values from 257 to 512, as said below
- input_proj: bfloat16 [3, 768, 768], P(None, 'dp', 'mp'), may hold values from -0.21875 to 0.21875
- output_proj: bfloat16 [768, 768], P('mp', 'dp'), may hold values from -0.875 to 0.875
- expand_weight: bfloat16 [768, 3072], P('dp', 'mp'), may hold values from -0.21875 to 0.21875
- shrink_weight: bfloat16 [3072, 768], P('mp', 'dp'), may hold values from -0.109375 to 0.109375
- head_bias: bfloat16 [2, 4, 192], P(None, 'mp', 'dp'), may hold values from -3 to 3
- expand_bias: bfloat16 [4, 768], P('mp', 'dp'), may hold values from -3 to 3
- row_params: float32 [6, 768], P(None, ('dp', 'mp')), may hold values from 0.25 to 1.75
- cotangent_long: bfloat16 [8, 1024, 768], P('dp', 'mp'), may hold values from -6 to 6
- cotangent_short: bfloat16 [16, 512, 768], P('dp', 'mp'), may hold values from -6 to 6
Outputs:
- result_long: bfloat16 [8, 1024, 768], P('dp', 'mp')
- result_short: bfloat16 [16, 512, 768], P('dp', 'mp')
- frames_grad_long: float32 [8, 1024, 768], P('dp', 'mp')
- frames_grad_short: float32 [16, 512, 768], P('dp', 'mp')
- input_proj_grad: float32 [3, 768, 768], P(None, 'dp', 'mp')
- output_proj_grad: float32 [768, 768], P('mp', 'dp')
- expand_grad: float32 [768, 3072], P('dp', 'mp')
- shrink_grad: float32 [3072, 768], P('mp', 'dp')
- head_bias_grad: float32 [2, 4, 192], P(None, 'mp', 'dp')
- expand_bias_grad: float32 [4, 768], P('mp', 'dp')
- row_params_grad: float32 [6, 768], P(None, ('dp', 'mp'))
Inputs may be any that keep to these rules, and one draw needn't show every extreme that they name: `length_long`: lengths of the long bucket; some clip has exactly 1024. `length_short`: lengths of the short bucket; some clip has exactly 512.
All inputs are finite; a program needn't handle non-finite values.
Results may differ from a plain program's by a relative error of at most 0.02.
Values may be sent and summed in bfloat16 or wider, within the bound.
No kernel may reach another device: no remote copies, remote signals or barrier semaphores. Data moves between devices by JAX's collectives and lax.ppermute only.
A program may use at most 128 MiB of HBM per device.

v0:
```python
import functools

import jax
import jax.numpy as jnp
from jax import lax
from jax.experimental import pallas as pl
from jax.experimental.pallas import tpu as pltpu
from jax.sharding import PartitionSpec as P

HEAD = 64
EPS = 1e-05
NEG_FILL = -1e30
SCALE = HEAD ** (-0.5)
N_MP = 4
PARTS = 1
CS = 0.3
WIDTH = 768
SMALL = 8
SHARED = 8
LANES = 128
Q_TILE = 256
F32 = jnp.float32
BF16 = jnp.bfloat16
NT = (((1,), (1,)), ((), ()))
NN = (((1,), (0,)), ((), ()))
TN = (((0,), (0,)), ((), ()))


def dot(left, right, dims):
    return lax.dot_general(left, right, dims, preferred_element_type=F32)


def mp_swap(value, step):
    return lax.ppermute(value, "mp", [(i, i ^ step) for i in range(N_MP)])


def dp_swap(value, target):
    size = lax.axis_size("dp")
    return lax.ppermute(value, "dp", [(i, target(i)) for i in range(size)])


def core_swap(value):
    return dp_swap(value, lambda i: i ^ 1)


def clip_blocks(long_rows, short_rows, core):
    block = short_rows.shape[1]
    keep = lax.dynamic_slice_in_dim(long_rows, core * block, block, 0)
    away = lax.dynamic_slice_in_dim(long_rows, (1 - core) * block, block, 0)
    back = core_swap(away)
    first = jnp.where(core == 0, keep, back)
    second = jnp.where(core == 0, back, keep)
    return jnp.stack([first, second, short_rows[0], short_rows[1]])


def clip_pieces(blocks, depth):
    return [
        lax.dynamic_index_in_dim(blocks, depth ^ step, 0, keepdims=False) for step in range(N_MP)
    ]


def to_clips(blocks, depth):
    pieces = clip_pieces(blocks, depth)
    return pieces[:1] + [mp_swap(pieces[step], step) for step in range(1, N_MP)]


def from_clips(rows):
    block = rows.shape[0] // N_MP
    parts = []
    for step in range(N_MP):
        piece = rows[step * block : (step + 1) * block]
        parts.append(piece if step == 0 else mp_swap(piece, step))
    return parts


def frames_of(parts, core, depth):
    blocks = jnp.stack(parts)
    first, second, short_a, short_b = (
        lax.dynamic_index_in_dim(blocks, depth ^ i, 0, keepdims=False) for i in range(N_MP)
    )
    keep = jnp.where(core == 0, first, second)
    away = jnp.where(core == 0, second, first)
    back = core_swap(away)
    low = jnp.where(core == 0, keep, back)
    high = jnp.where(core == 0, back, keep)
    return jnp.concatenate([low, high], axis=0)[None], jnp.stack([short_a, short_b])


def flip(index, late):
    return index ^ ((4 if late else 2) if index % 2 == 0 else (2 if late else 4))


def block_table(mine, size):
    if size != 8:
        return jnp.zeros((1,), jnp.int32)
    early = jnp.where(mine % 2 == 0, 2, 4)
    late = 6 - early
    relative = [0, early, late, 6, 1, 1 ^ late, 1 ^ early, 7]
    return jnp.stack([mine ^ r for r in relative]).astype(jnp.int32)


def early(i):
    return flip(i, False)


def late(i):
    return flip(i, True)


def across(i):
    return i ^ 6


def tie(*values):
    return lax.optimization_barrier(values)


def swap_plane(plane):
    return plane + [core_swap(piece) for piece in plane]


def to_slab(parts):
    return jnp.concatenate(parts, axis=1)


def mp_gather(shard):
    return [shard] + [mp_swap(shard, step) for step in range(1, N_MP)]


def goes_on(terms):
    half = terms[0].shape[0] // 2
    return sum(term[half:].astype(F32) for term in terms).astype(BF16)


def stays(terms, back):
    half = terms[0].shape[0] // 2
    return [term[:half] for term in terms] + [back]


def mp_away(parts):
    return [mp_swap(parts[step].astype(BF16), step) for step in range(1, N_MP)]


def mp_total(own, backs):
    for back in backs:
        own = own + back.astype(F32)
    return own


def blocks_of(pieces):
    step = pieces[0].shape[0]
    return [(p, k * step) for p in pieces for k in range(p.shape[0] // step)]


def block_rows(pieces):
    return WIDTH // len(blocks_of(pieces))


class Weights:
    def __init__(self, pieces, table, held, sems, lo, tile):
        self.held, self.tile = held, tile
        cols, parts = held.shape[2], sems.shape[0]
        self.span, self.copies = cols // parts, []
        for t in range(parts):
            row = []
            for k, (piece, first) in enumerate(blocks_of(pieces)):
                copy = pltpu.make_async_copy(
                    piece.at[pl.ds(first, held.shape[1]), pl.ds(lo + t * self.span, self.span)],
                    held.at[table[k], :, pl.ds(t * self.span, self.span)],
                    sems.at[t, k],
                )
                copy.start()
                row.append(copy)
            self.copies.append(row)
        self.waited = 0

    def whole(self):
        for row in self.copies[self.waited :]:
            for copy in row:
                copy.wait()
        self.waited = len(self.copies)

    def at(self, at):
        count, rows, _ = self.held.shape
        return self.held[:, :, pl.ds(at, self.tile)].reshape(count * rows, self.tile)

    def get(self, t):
        at = t * self.tile
        while self.waited * self.span < at + self.tile:
            for copy in self.copies[self.waited]:
                copy.wait()
            self.waited += 1
        count, rows, _ = self.held.shape
        return self.held[:, :, at : at + self.tile].reshape(count * rows, self.tile)


def weight_scratch(pieces, cols, parts=1):
    return [
        pltpu.VMEM((len(blocks_of(pieces)), block_rows(pieces), cols), BF16),
        pltpu.SemaphoreType.DMA((parts, len(blocks_of(pieces)))),
    ]


def grad_shapes(pieces, cols, extra=0):
    count, rows = len(blocks_of(pieces)), block_rows(pieces)
    if count == 1:
        return [jax.ShapeDtypeStruct((1, rows, cols), F32)]
    return [jax.ShapeDtypeStruct((count // 2, rows + extra, cols), BF16)] * 2


def turn_scratch(pieces, rows):
    return [pltpu.VMEM((len(blocks_of(pieces)), block_rows(pieces), rows), BF16)] * 2


def turn(value, table, plain, turned):
    plain[...] = value.T.reshape(plain.shape)
    for r in range(plain.shape[0]):
        turned[r] = plain[table[r]]


def stage_scratch(pieces, cols):
    return [
        pltpu.VMEM((g.shape[0], block_rows(pieces), cols), g.dtype)
        for g in grad_shapes(pieces, cols)
    ]


def store_grad(turned, right, stages, at):
    count, rows, _ = turned.shape
    grad = dot(turned[...].reshape(count * rows, -1), right, NN)
    half, cols = count // len(stages), right.shape[1]
    for r in range(count):
        stage = stages[r // half]
        part = grad[r * rows : (r + 1) * rows].astype(stage.dtype)
        stage[r % half, :rows, pl.ds(at, cols)] = part


def grad_copies(stages, outs, at, cols, sems, first):
    return [
        pltpu.make_async_copy(
            stage.at[:, :, pl.ds(at, cols)],
            out.at[:, pl.ds(0, stage.shape[1]), pl.ds(at, cols)],
            sems.at[first + i],
        )
        for i, (stage, out) in enumerate(zip(stages, outs))
    ]


def start_all(copies):
    for copy in copies:
        copy.start()


def wait_all(copies):
    for copy in copies:
        copy.wait()


class Writes:
    def __init__(self, sems):
        self.sems, self.copies = sems, []

    def start(self, source, target):
        copy = pltpu.make_async_copy(source, target, self.sems.at[len(self.copies)])
        copy.start()
        self.copies.append(copy)

    def finish(self):
        for copy in self.copies:
            copy.wait()


class Reads:
    def __init__(self, sources, targets, sems):
        self.targets, self.copies = targets, []
        for i, (source, target) in enumerate(zip(sources, targets)):
            copy = pltpu.make_async_copy(source, target, sems.at[i])
            copy.start()
            self.copies.append(copy)

    def get(self, i):
        self.copies[i].wait()
        return self.targets[i]


def read_scratch(arrays):
    return [pltpu.VMEM(a.shape, a.dtype) for a in arrays] + [
        pltpu.SemaphoreType.DMA((len(arrays),))
    ]


def cost(micros):
    return pl.CostEstimate(
        flops=int(micros * 1.1e9 * CS), bytes_accessed=int(micros * 1e5 * CS), transcendentals=0
    )


def call(body, name, micros, outs, arrays, table, pieces, scratch, far=0):
    vmem = pl.BlockSpec(memory_space=pltpu.VMEM)
    away = pl.BlockSpec(memory_space=pl.ANY)
    return pl.pallas_call(
        body,
        out_shape=tuple(outs),
        in_specs=[pl.BlockSpec(memory_space=pltpu.SMEM)]
        + [vmem] * len(arrays)
        + [away] * len(pieces),
        out_specs=(vmem,) * (len(outs) - far) + (away,) * far,
        scratch_shapes=scratch,
        compiler_params=pltpu.CompilerParams(vmem_limit_bytes=60 << 20),
        cost_estimate=cost(micros),
        name=name,
    )(table, *arrays, *pieces)


def like(shape, kind):
    return jax.ShapeDtypeStruct(shape, kind)


def attend_kernel(q_ref, k_ref, v_ref, kp_ref, vp_ref, bias_ref, o_ref, lse_ref):
    rows = q_ref.shape[0]
    keys = jnp.concatenate([k_ref[...], kp_ref[...]], axis=0)
    values = jnp.concatenate([v_ref[...], vp_ref[...]], axis=0)
    bias = bias_ref[...]
    tile = min(rows, Q_TILE)
    low = lax.broadcasted_iota(jnp.int32, (tile, LANES), 1) < HEAD
    for start in range(0, rows, tile):
        q = q_ref[start : start + tile, :]
        outs, logs = [], []
        for half in range(2):
            here = low if half == 0 else ~low
            q_here = jnp.where(here, q, jnp.zeros_like(q))
            scores = dot(q_here, keys, NT) + bias
            top = jnp.max(scores, axis=-1, keepdims=True)
            raised = jnp.exp(scores - top)
            total = jnp.sum(raised, axis=-1, keepdims=True)
            mixed = dot(raised.astype(BF16), values, NN)
            outs.append(mixed / total)
            logs.append(top + jnp.log(total))
        o_ref[start : start + tile, :] = jnp.where(low, outs[0], outs[1]).astype(BF16)
        lse_ref[start : start + tile, :] = jnp.where(low, logs[0], logs[1])


def attend(qkv, kv_other, bias):
    rows, width = qkv.shape[0], qkv.shape[1] // 3
    pairs = width // LANES
    spec = lambda base: pl.BlockSpec((rows, LANES), lambda p: (0, base + p))
    return pl.pallas_call(
        attend_kernel,
        out_shape=(
            jax.ShapeDtypeStruct((rows, width), BF16),
            jax.ShapeDtypeStruct((rows, width), F32),
        ),
        grid=(pairs,),
        in_specs=[
            spec(0),
            spec(pairs),
            spec(2 * pairs),
            spec(0),
            spec(pairs),
            pl.BlockSpec((1, 2 * rows), lambda p: (0, 0)),
        ],
        out_specs=(spec(0), spec(0)),
        compiler_params=pltpu.CompilerParams(vmem_limit_bytes=56 << 20),
        cost_estimate=cost(15),
        name="attend",
    )(qkv, qkv, qkv, kv_other, kv_other, bias)


def attend_back_kernel(
    q_ref, k_ref, v_ref, kp_ref, vp_ref, bias_ref, o_ref, lse_ref, do_ref,
    dq_ref, own_ref, other_ref,
):
    rows = q_ref.shape[0]
    keys = jnp.concatenate([k_ref[...], kp_ref[...]], axis=0)
    values = jnp.concatenate([v_ref[...], vp_ref[...]], axis=0)
    bias = bias_ref[...]
    tile = min(rows, Q_TILE)
    low = lax.broadcasted_iota(jnp.int32, (tile, LANES), 1) < HEAD
    dk = jnp.zeros((LANES, 2 * rows), F32)
    dv = jnp.zeros((LANES, 2 * rows), F32)
    for start in range(0, rows, tile):
        at = slice(start, start + tile)
        q, do = q_ref[at, :], do_ref[at, :]
        product = o_ref[at, :].astype(F32) * do.astype(F32)
        lse = lse_ref[at, :]
        outs = []
        for half in range(2):
            here = low if half == 0 else ~low
            q_here = jnp.where(here, q, jnp.zeros_like(q))
            do_here = jnp.where(here, do, jnp.zeros_like(do))
            inner = jnp.sum(jnp.where(here, product, 0.0), axis=-1, keepdims=True)
            log = lse[:, half * HEAD : half * HEAD + 1]
            soft = jnp.exp(dot(q_here, keys, NT) + bias - log)
            grad = (soft * (dot(do_here, values, NT) - inner)).astype(BF16)
            outs.append(dot(grad, keys, NN))
            dk = dk + dot(q_here, grad, TN)
            dv = dv + dot(do_here, soft.astype(BF16), TN)
        dq_ref[at, :] = (jnp.where(low, outs[0], outs[1]) * SCALE).astype(BF16)
    for i, value in enumerate((dk.T, dv.T)):
        at = slice(i * LANES, (i + 1) * LANES)
        own_ref[:, at] = value[:rows]
        other_ref[:, at] = value[rows:].astype(BF16)


def attend_back(qkv, kv_other, bias, out, lse, grad_out, first, count):
    rows, width = out.shape
    pairs = width // LANES
    spec = lambda base: pl.BlockSpec((rows, LANES), lambda p: (0, base + first + p))
    result = lambda cols: pl.BlockSpec((rows, cols), lambda p: (0, p))
    return pl.pallas_call(
        attend_back_kernel,
        out_shape=(
            jax.ShapeDtypeStruct((rows, count * LANES), BF16),
            jax.ShapeDtypeStruct((rows, 2 * count * LANES), F32),
            jax.ShapeDtypeStruct((rows, 2 * count * LANES), BF16),
        ),
        grid=(count,),
        in_specs=[
            spec(0),
            spec(pairs),
            spec(2 * pairs),
            spec(0),
            spec(pairs),
            pl.BlockSpec((1, 2 * rows), lambda p: (0, 0)),
            spec(0),
            spec(0),
            spec(0),
        ],
        out_specs=(result(LANES), result(2 * LANES), result(2 * LANES)),
        compiler_params=pltpu.CompilerParams(vmem_limit_bytes=56 << 20),
        cost_estimate=cost(3 * count),
        name="attend_back",
    )(qkv, qkv, qkv, kv_other, kv_other, bias, out, lse, grad_out)


def gelu_parts(v):
    cdf = 0.5 * (1.0 + lax.erf(v * (2.0 ** -0.5)))
    pdf = jnp.exp(-0.5 * v * v) * 0.3989422804014327
    return v * cdf, cdf + v * pdf


def norm(values):
    center = values - jnp.mean(values, axis=-1, keepdims=True)
    inv_dev = lax.rsqrt(jnp.mean(center * center, axis=-1, keepdims=True) + EPS)
    return center * inv_dev, inv_dev


def norm_back(scaled, normed, inv_dev):
    return inv_dev * (
        scaled
        - jnp.mean(scaled, axis=-1, keepdims=True)
        - normed * jnp.mean(scaled * normed, axis=-1, keepdims=True)
    )


def total(value):
    return jnp.sum(value, axis=0, keepdims=True)


def join(parts, starts, size, micros):
    rows, cols = parts[0].shape[0], len(starts) * len(parts) * size

    def body(*refs):
        parts, out = refs[:-1], refs[-1]
        at = 0
        for start in starts:
            for part in parts:
                out[:, at : at + size] = part[:, start : start + size]
                at += size

    vmem = pl.BlockSpec(memory_space=pltpu.VMEM)
    return pl.pallas_call(
        body,
        out_shape=like((rows, cols), parts[0].dtype),
        in_specs=[vmem] * len(parts),
        out_specs=vmem,
        cost_estimate=cost(micros),
        name="join",
    )(*parts)


def project(x_parts, head_row, table, pieces):
    block, width = x_parts[0].shape
    rows = block * len(x_parts)
    n = len(pieces)

    def body(table, *refs):
        part_refs, bias_ref, refs = refs[:N_MP], refs[N_MP], refs[N_MP + 1 :]
        pieces, (x_ref, qkv_ref, kv_ref, held, sems) = refs[:n], refs[n:]
        weights = Weights(pieces, table, held, sems, 0, width)
        for i, part in enumerate(part_refs):
            x_ref[i * block : (i + 1) * block, :] = part[...]
        x = x_ref[...]
        for i in range(3):
            value = dot(x, weights.get(i), NN) + bias_ref[:, i * width : (i + 1) * width]
            value = value.astype(BF16)
            if i == 0:
                value = (value.astype(F32) * SCALE).astype(BF16)
            else:
                kv_ref[:, (i - 1) * width : i * width] = value
            qkv_ref[:, i * width : (i + 1) * width] = value

    return call(
        body,
        "project",
        7,
        [
            like((rows, width), BF16),
            like((rows, 3 * width), BF16),
            like((rows, 2 * width), BF16),
        ],
        list(x_parts) + [head_row],
        table,
        pieces,
        weight_scratch(pieces, 3 * width, 3),
    )


def feed(x, mixed, cot_parts, smalls, small_row, table, out_pieces, feed_pieces):
    rows, width = x.shape
    hidden = feed_pieces[0].shape[1] // 2
    count = 6
    tile = hidden // count
    cols = hidden + width
    n_out, n_up, n = len(out_pieces), len(feed_pieces), len(smalls)
    down_grads = grad_shapes(feed_pieces, hidden)
    mid_grads = grad_shapes(feed_pieces, cols, SHARED)
    g = len(mid_grads)

    def body(table, x_ref, mixed_ref, *refs):
        cot_far, small_far, refs = refs[:N_MP], refs[N_MP : N_MP + n], refs[N_MP + n :]
        out_p, up_p = refs[:n_out], refs[n_out : n_out + n_up]
        refs = refs[n_out + n_up :]
        shared_ref, result_out, da_out, do_out = refs[:4]
        down_outs, mid_outs, refs = refs[4 : 4 + g], refs[4 + g : 4 + 2 * g], refs[4 + 2 * g :]
        w_out, sems_out, w_up, sems_up, w_down, sems_down = refs[:6]
        plain, turned, plain_h, turned_h = refs[6:10]
        small_ref, cot_ref, read_sems = refs[10:13]
        n1_ref, dz_ref, h_ref, act_ref, slope_ref, result_ref, low_ref, do_ref = refs[13:21]
        down_stages, mid_stages = refs[21 : 21 + g], refs[21 + g : 21 + 2 * g]
        shared_low, sems, grad_sems, up_b_ref = refs[21 + 2 * g :]
        out_w = Weights(out_p, table, w_out, sems_out, 3 * width, width)
        smalls = [small.at[pl.ds(small_row, SMALL)] for small in small_far]
        reads = Reads(smalls, [small_ref.at[i] for i in range(n)], read_sems)
        up_w = Weights(up_p, table, w_up, sems_up, 0, tile)
        down_w = Weights(up_p, table, w_down, sems_down, hidden, tile)
        block = rows // N_MP
        cots = Reads(
            cot_far,
            [cot_ref.at[pl.ds(i * block, block)] for i in range(N_MP)],
            read_sems.at[pl.ds(n, N_MP)],
        )
        writes = Writes(sems)

        attention = dot(mixed_ref[...], out_w.get(0), NT)
        for i in range(n):
            reads.get(i)
        small = jnp.sum(small_ref[...].astype(F32), axis=0)
        row_vals = sum(small[:, i * width : (i + 1) * width] for i in range(2 * N_MP))
        row = lambda i: row_vals[i : i + 1, :]
        up_b = small[6:7, :hidden]
        n1, r1 = norm(x_ref[...].astype(F32) + attention + row(0))
        n1_ref[...] = n1
        h_ref[...] = (n1 * row(1) + row(2)).astype(BF16)
        up_b_ref[...] = up_b
        dz_ref[...] = jnp.zeros_like(dz_ref)
        up_w.whole()
        down_w.whole()

        @pl.loop(0, count)
        def _(t):
            at = pl.multiple_of(t * tile, tile)
            u = dot(h_ref[...], up_w.at(at), NN)
            act, slope = gelu_parts(u + up_b_ref[:, pl.ds(at, tile)])
            act_ref[:, pl.ds(at, tile)] = act.astype(BF16)
            slope_ref[:, pl.ds(at, tile)] = slope.astype(BF16)
            dz_ref[...] += dot(act_ref[:, pl.ds(at, tile)], down_w.at(at), NT)

        feed = dz_ref[...]
        h = n1_ref[...] * row(1) + row(2)
        n2, r2 = norm(h + feed + row(3))
        result_ref[...] = (n2 * row(4) + row(5)).astype(BF16)
        writes.start(result_ref, result_out)
        for i in range(N_MP):
            cots.get(i)
        gy = cot_ref[...].astype(F32)
        dz = norm_back(gy * row(4), n2, r2)
        dz_ref[...] = dz
        low_ref[...] = dz.astype(BF16)
        sums = [total(dz), total(gy * n2), total(gy)]

        turn(low_ref[...], table, plain, turned)
        turn(h_ref[...], table, plain_h, turned_h)
        shared_ref[...] = jnp.zeros_like(shared_ref)
        def tile_copies(t):
            at = t * tile if isinstance(t, int) else pl.multiple_of(t * tile, tile)
            down = grad_copies(down_stages, down_outs, at, tile, grad_sems, 2 * g * t)
            return down + grad_copies(mid_stages, mid_outs, at, tile, grad_sems, 2 * g * t + g)

        @pl.loop(0, count)
        def _(t):
            at = pl.multiple_of(t * tile, tile)
            dact = dot(low_ref[...], down_w.at(at), NN)
            store_grad(turned, act_ref[:, pl.ds(at, tile)], down_stages, at)
            du = (dact * slope_ref[:, pl.ds(at, tile)].astype(F32)).astype(BF16)
            shared_ref[0:1, pl.ds(at, tile)] = total(du.astype(F32))
            dz_ref[...] += dot(du, up_w.at(at), NT)
            store_grad(turned_h, du, mid_stages, at)
            start_all(tile_copies(t))

        dh = dz_ref[...]
        n1 = n1_ref[...]
        da = norm_back(dh * row(1), n1, r1)
        dz_ref[...] = da
        writes.start(dz_ref, da_out)
        low_ref[...] = da.astype(BF16)
        do_ref[...] = dot(low_ref[...], out_w.get(0), NN).astype(BF16)
        writes.start(do_ref, do_out)
        sums = [total(da), total(dh * n1), total(dh)] + sums
        for j in range(hidden // width):
            for i, value in enumerate(sums):
                shared_ref[1 + i : 2 + i, j * width : (j + 1) * width] = value
        if g > 1:
            shared_low[...] = shared_ref[...].astype(BF16)
            for out in mid_outs:
                for r in range(out.shape[0]):
                    writes.start(shared_low, out.at[r, pl.ds(block_rows(feed_pieces), SHARED)])
        turn(low_ref[...], table, plain, turned)
        store_grad(turned, mixed_ref[...], mid_stages, hidden)
        last = grad_copies(mid_stages, mid_outs, hidden, width, grad_sems, 2 * g * count)
        start_all(last)
        for t in range(count):
            wait_all(tile_copies(t))
        wait_all(last)
        writes.finish()

    near = [((rows, width), F32)] * 2 + [((rows, width), BF16)]
    near += [((rows, hidden), BF16)] * 2 + [((rows, width), BF16)] * 3
    return call(
        body,
        "feed",
        33,
        [
            like((SHARED, cols), F32),
            like((rows, width), BF16),
            like((rows, width), F32),
            like((rows, width), BF16),
        ]
        + down_grads
        + mid_grads,
        [x, mixed],
        table,
        list(cot_parts) + list(smalls) + list(out_pieces) + list(feed_pieces),
        weight_scratch(out_pieces, width)
        + weight_scratch(feed_pieces, hidden) * 2
        + turn_scratch(feed_pieces, rows) * 2
        + [
            pltpu.VMEM((n, SMALL, 2 * hidden), BF16),
            pltpu.VMEM((rows, width), BF16),
            pltpu.SemaphoreType.DMA((n + N_MP,)),
        ]
        + [pltpu.VMEM(*spec) for spec in near]
        + stage_scratch(feed_pieces, hidden)
        + stage_scratch(feed_pieces, cols)
        + [
            pltpu.VMEM((SHARED, cols), BF16),
            pltpu.SemaphoreType.DMA((3 + n_up,)),
            pltpu.SemaphoreType.DMA((g * (2 * count + 1),)),
            pltpu.VMEM((1, hidden), F32),
        ],
        far=3 + 2 * g,
    )


def project_back(da, parts, table, pieces):
    rows, width = da.shape
    n = len(pieces)
    flat = [value for part in parts for value in part]

    def body(table, da_ref, *refs):
        part_refs, refs = refs[: len(flat)], refs[len(flat) :]
        pieces, (out_ref, dqkv_ref, held, sems) = refs[:n], refs[n:]
        weights = Weights(pieces, table, held, sems, 0, width)
        pair = 0
        for i in range(0, len(flat), 3):
            q_ref, own_ref, back_ref = part_refs[i : i + 3]
            cols = q_ref.shape[1]
            dqkv_ref[:, pair * LANES : pair * LANES + cols] = q_ref[...]
            for p in range(cols // LANES):
                for which in range(2):
                    at = slice((2 * p + which) * LANES, (2 * p + which + 1) * LANES)
                    to = (which + 1) * width + (pair + p) * LANES
                    value = own_ref[:, at] + back_ref[:, at].astype(F32)
                    dqkv_ref[:, to : to + LANES] = value.astype(BF16)
            pair += cols // LANES
        value = da_ref[...]
        for i in range(3):
            value = value + dot(dqkv_ref[:, i * width : (i + 1) * width], weights.get(i), NT)
        out_ref[...] = value.astype(BF16)

    return call(
        body,
        "project_back",
        9,
        [like((rows, width), BF16), like((rows, 3 * width), BF16)],
        [da] + flat,
        table,
        pieces,
        weight_scratch(pieces, 3 * width, 3),
    )


def project_grads(x, dqkv, table, pieces):
    rows, width = x.shape
    grads = grad_shapes(pieces, 3 * width, SHARED)
    g = len(grads)

    def body(table, x_ref, dqkv_ref, *refs):
        shared_ref, grad_outs, refs = refs[0], refs[1 : 1 + g], refs[1 + g :]
        plain, turned = refs[:2]
        stages, shared_low, sems = refs[2 : 2 + g], refs[2 + g], refs[3 + g]
        writes = Writes(sems.at[pl.ds(3 * g, len(blocks_of(pieces)))])
        turn(x_ref[...], table, plain, turned)

        @pl.loop(0, 3)
        def _(i):
            at = pl.multiple_of(i * width, width)
            store_grad(turned, dqkv_ref[:, pl.ds(at, width)], stages, at)
            start_all(grad_copies(stages, grad_outs, at, width, sems, g * i))

        shared_ref[...] = jnp.zeros_like(shared_ref)
        shared_ref[0:1, :] = total(dqkv_ref[...].astype(F32))
        if g > 1:
            shared_low[...] = shared_ref[...].astype(BF16)
            for out in grad_outs:
                for r in range(out.shape[0]):
                    writes.start(shared_low, out.at[r, pl.ds(block_rows(pieces), SHARED)])
        for i in range(3):
            wait_all(grad_copies(stages, grad_outs, i * width, width, sems, g * i))
        writes.finish()

    return call(
        body,
        "project_grads",
        7,
        [like((SHARED, 3 * width), F32)] + grads,
        [x, dqkv],
        table,
        [],
        turn_scratch(pieces, rows)
        + stage_scratch(pieces, 3 * width)
        + [
            pltpu.VMEM((SHARED, 3 * width), BF16),
            pltpu.SemaphoreType.DMA((3 * g + len(blocks_of(pieces)),)),
        ],
        far=g,
    )


def at_column(values, rows, width, column):
    return lax.dynamic_update_slice(jnp.zeros((rows, width), values.dtype), values, (0, column))


def small_block(row_params, expand_bias, mine, depth):
    high = lax.reduce_precision(row_params, 8, 7)
    column = (mine * N_MP + depth) * row_params.shape[1]
    high_low = [
        at_column(part.astype(BF16), 6, WIDTH, column) for part in (high, row_params - high)
    ]
    bias = at_column(expand_bias, 2, 2 * WIDTH, mine * expand_bias.shape[1])
    return jnp.concatenate([jnp.concatenate(high_low, axis=1), bias])


def key_bias(length_long, length_short, block, core, depth):
    lengths = jnp.concatenate([length_long, length_short])
    other = core_swap(lengths)
    longs = jnp.where(core == 0, jnp.stack([lengths[0], other[0]]), jnp.stack([other[0], lengths[0]]))
    length = jnp.concatenate([longs, lengths[1:]])[depth]
    is_long = depth < 2
    place = lax.broadcasted_iota(jnp.int32, (1, 2 * N_MP * block), 1)
    row = place % (N_MP * block)
    is_own = place < N_MP * block
    source = (row // block) ^ depth
    whose = jnp.where(is_own, core, 1 - core)
    frame = row % block + jnp.where(is_long, (2 * source + whose) * block, source * block)
    counted = (frame < length) & (is_own | is_long)
    return jnp.where(counted, 0.0, NEG_FILL).astype(F32)


def on_device(
    frames_long,
    frames_short,
    length_long,
    length_short,
    input_proj,
    output_proj,
    expand_weight,
    shrink_weight,
    head_bias,
    expand_bias,
    row_params,
    cotangent_long,
    cotangent_short,
):
    mine = lax.axis_index("dp")
    depth = lax.axis_index("mp")
    n_dp = lax.axis_size("dp")
    fast = n_dp == 8
    core = mine % 2
    block = frames_short.shape[1]
    shard, group = input_proj.shape[1:]
    units = expand_weight.shape[1]
    width = group * N_MP
    hidden = units * N_MP
    table = block_table(mine, n_dp)

    joined = jnp.concatenate(
        [input_proj[0], input_proj[1], input_proj[2], output_proj.T], axis=1
    )
    heads = at_column(head_bias[:, 0], SMALL, WIDTH, mine * head_bias.shape[2])
    attn_parts = mp_gather(jnp.concatenate([joined, heads]))
    x_blocks = clip_blocks(frames_long[0], frames_short, core)
    cot_blocks = clip_blocks(cotangent_long[0], cotangent_short, core)
    bias = key_bias(length_long, length_short, block, core, depth)
    feed_shard = jnp.concatenate(
        [
            jnp.concatenate([expand_weight, shrink_weight.T], axis=1),
            small_block(row_params, expand_bias, mine, depth),
        ]
    )
    *attn_parts, feed_shard, bias, x_blocks, cot_blocks = tie(
        *attn_parts, feed_shard, bias, x_blocks, cot_blocks
    )
    order = [p[:shard, i * group : (i + 1) * group] for i in range(4) for p in attn_parts]
    attn_slab = jnp.concatenate([to_slab(order), to_slab([p[shard:] for p in attn_parts])])
    feed_parts = mp_gather(feed_shard)
    feed_order = [p[:, i * units : (i + 1) * units] for i in range(2) for p in feed_parts]
    if fast:
        attn_p = [attn_slab] + [dp_swap(attn_slab, to) for to in (early, late, across)]
        x_pieces = clip_pieces(x_blocks, depth)
        attn_p += [core_swap(piece) for piece in attn_p]
        both = tie(*attn_p, *x_pieces, *feed_order)
        attn_p, x_pieces, feed_order = both[:8], both[8:12], both[12:]
        feed_slab = to_slab(feed_order)
        feed_one = dp_swap(feed_slab, early)
        feed_two = dp_swap(feed_slab, late)
        x_parts = [x_pieces[0]] + [mp_swap(x_pieces[i], i) for i in range(1, N_MP)]
        *x_parts, cot_blocks, own_slab = tie(*x_parts, cot_blocks, feed_slab)
        heads = sum(p[shard:].astype(F32) for p in attn_p)
    else:
        x_parts = to_clips(x_blocks, depth)
        gather = lambda slab: lax.all_gather(slab, "dp", axis=0)
        whole = gather(attn_slab)
        heads = jnp.sum(whole[:, shard:].astype(F32), axis=0)
        attn_p = [whole[:, :shard].reshape(width, 4 * width)]
        whole = gather(to_slab(feed_order))
        small = jnp.sum(whole[:, shard:].astype(F32), axis=0)
        feed_p = [whole[:, :shard].reshape(width, 2 * hidden)]
    cot_parts = to_clips(cot_blocks, depth)
    heads = jnp.concatenate(
        [heads[:2, i * width : i * width + group] for i in range(N_MP)], axis=1
    )
    head_row = jnp.concatenate([heads[:1], jnp.zeros_like(heads[:1]), heads[1:]], axis=1)

    x, qkv, kv = project(x_parts, head_row, table, attn_p)
    if fast:
        kv, feed_one, feed_two, cot_parts[3], own_slab = tie(
            kv, feed_one, feed_two, cot_parts[3], core_swap(own_slab)
        )
    kv_other = core_swap(kv)
    if fast:
        feed_three = dp_swap(feed_one, late)
        feed_p = [feed_slab, feed_one, feed_two]
        backs = [own_slab] + [core_swap(piece) for piece in feed_p[1:]]
    mixed, lse = attend(qkv, kv_other, bias)
    if fast:
        mixed, feed_three, *both = tie(mixed, feed_three, *backs, *cot_parts)
        backs, cot_parts = both[:3], both[3:]
        feed_p = feed_p + [feed_three] + backs + [core_swap(feed_three)]
        smalls, small_row = feed_p, shard
    else:
        smalls, small_row = [small.astype(BF16)], 0
    outs = feed(x, mixed, cot_parts, smalls, small_row, table, attn_p, feed_p)
    mid_shared, result, da, do, *grads = outs
    g_down, g_mid = grads[: len(grads) // 2], grads[len(grads) // 2 :]

    def by_group_of(value, sizes):
        starts = [N_MP * sum(sizes[:i]) for i in range(len(sizes))]
        return [
            jnp.concatenate(
                [value[:, a + j * n : a + (j + 1) * n] for a, n in zip(starts, sizes)], axis=1
            )
            for j in range(N_MP)
        ]

    def last_sum(terms):
        return sum(term[0].astype(F32) for term in terms)

    result_parts = from_clips(result)
    if fast:
        b_down, b_mid = core_swap(g_down[1]), core_swap(g_mid[1])
    pairs = width // LANES
    first = pairs // 2
    dq_a, own_a, other_a = attend_back(qkv, kv_other, bias, mixed, lse, do, 0, first)
    if fast:
        other_a, b_down, b_mid, result_parts[3] = tie(other_a, b_down, b_mid, result_parts[3])
        t_down = [g_down[0], b_down]
        a_down = goes_on(t_down)
        do, a_down = tie(do, a_down)
        b_down = dp_swap(a_down, late)
        t_mid = [g_mid[0], b_mid]
        a_mid = goes_on(t_mid)
        do, a_mid = tie(do, a_mid)
        b_mid = dp_swap(a_mid, late)
    back_a = core_swap(other_a)
    dq_b, own_b, other_b = attend_back(
        qkv, kv_other, bias, mixed, lse, do, first, pairs - first
    )
    if fast:
        other_b, back_a, *result_parts = tie(other_b, back_a, *result_parts)
    back_b = core_swap(other_b)
    parts = [(dq_a, own_a, back_a), (dq_b, own_b, back_b)]
    frames_grad, dqkv = project_back(da, parts, table, attn_p)
    grad_parts = from_clips(frames_grad)
    if fast:
        dqkv, b_down, b_mid = tie(dqkv, b_down, b_mid)
        t_down, t_mid = stays(t_down, b_down), stays(t_mid, b_mid)
        a_down, a_mid = goes_on(t_down), goes_on(t_mid)
        dqkv, a_down, a_mid = tie(dqkv, a_down, a_mid)
        b_down = dp_swap(a_down, early)
        b_mid = dp_swap(a_mid, early)
    attn_shared, *g_attn = project_grads(x, dqkv, table, attn_p)
    if fast:
        both = tie(*g_attn, b_down, b_mid, *grad_parts)
        g_attn, b_down, b_mid, grad_parts = both[:2], both[2], both[3], both[4:]
        b_attn = core_swap(g_attn[1])
        s_down = by_group_of(last_sum(stays(t_down, b_down)), [units])
        t_attn = [g_attn[0], b_attn]
        a_attn = goes_on(t_attn)
        a_attn, *s_down = tie(a_attn, *s_down)
        b_attn = dp_swap(a_attn, late)
        z_down = mp_away(s_down)
        s_mid = by_group_of(last_sum(stays(t_mid, b_mid)), [units, group])
        b_attn, *z_down = tie(b_attn, *z_down)
        t_attn = stays(t_attn, b_attn)
        a_attn = goes_on(t_attn)
        z_mid = mp_away(s_mid)
        b_attn, *both = tie(dp_swap(a_attn, early), *z_mid, *result_parts)
        z_mid, result_parts = both[: N_MP - 1], both[N_MP - 1 :]
        s_attn = last_sum(stays(t_attn, b_attn))
    else:
        scatter = lambda g: lax.psum_scatter(g[0][0], "dp", scatter_dimension=0, tiled=True)
        s_down = by_group_of(scatter(g_down), [units])
        z_down = mp_away(s_down)
        s_mid = jnp.concatenate([scatter(g_mid), lax.psum(mid_shared, "dp")])
        s_mid = by_group_of(s_mid, [units, group])
        z_mid = mp_away(s_mid)
        s_attn = jnp.concatenate([scatter(g_attn), lax.psum(attn_shared, "dp")])
    s_attn = by_group_of(s_attn, [group] * 3)
    grad_long, grad_short = frames_of(grad_parts, core, depth)
    result_long, result_short = frames_of(result_parts, core, depth)
    attn_share = mp_total(s_attn[0], mp_away(s_attn))
    down_share = mp_total(s_down[0], z_down).T
    mid_share = mp_total(s_mid[0], z_mid)
    up_share = mid_share[:shard, :units]
    output_share = mid_share[:shard, units:].T
    input_share = jnp.stack(
        [attn_share[:shard, i * group : (i + 1) * group] for i in range(3)]
    )
    up_cols, head_cols, row_cols = units // n_dp, group // n_dp, width // (n_dp * N_MP)
    rank = mine * N_MP + depth
    up_b_share = lax.dynamic_slice(mid_share, (shard, mine * up_cols), (1, up_cols))
    row_share = lax.dynamic_slice(mid_share, (shard + 1, rank * row_cols), (6, row_cols))
    head_share = jnp.stack(
        [
            lax.dynamic_slice(attn_share, (shard, at + mine * head_cols), (1, head_cols))
            for at in (0, 2 * group)
        ]
    )
    return (
        result_long,
        result_short,
        grad_long.astype(F32),
        grad_short.astype(F32),
        input_share,
        output_share,
        up_share,
        down_share,
        head_share,
        up_b_share,
        row_share,
    )


def solution(mesh):
    return jax.shard_map(
        on_device,
        mesh=mesh,
        in_specs=(
            P("dp", "mp", None),
            P("dp", "mp", None),
            P("dp"),
            P("dp"),
            P(None, "dp", "mp"),
            P("mp", "dp"),
            P("dp", "mp"),
            P("mp", "dp"),
            P(None, "mp", "dp"),
            P("mp", "dp"),
            P(None, ("dp", "mp")),
            P("dp", "mp", None),
            P("dp", "mp", None),
        ),
        out_specs=(
            P("dp", "mp", None),
            P("dp", "mp", None),
            P("dp", "mp", None),
            P("dp", "mp", None),
            P(None, "dp", "mp"),
            P("mp", "dp"),
            P("dp", "mp"),
            P("mp", "dp"),
            P(None, "mp", "dp"),
            P("mp", "dp"),
            P(None, ("dp", "mp")),
        ),
        check_vma=False,
    )
```

profile of v0, /device:TPU:0, one launch (start us, length us, event | category | flops | bytes accessed | tf_op | source)
XLA Modules:
  0.0 302.0 jit_solution(4587057015419667677)
XLA Ops:
  4.2 5.1 %collective-permute-start.2 = (bf16[104,768]{1,0:T(8,128)(2,1)S(1)}, bf16[104,768]{1,0:T(8,128)(2,1)S(1)}, u32[]{:S(2)}, u32[]{:S(2)}) collective-permute-start(bf16[104,768]{1,0:T(8,128)(2,1)S(1)} %pad_maximum_fusion.10), channel_id=1, source_target_pairs={{0,3},{1,2},{2,1},{3,0},{4,7},{5,6},{6,5},{7,4},{8,11},{9,10},{10,... | collective-permute-start | bytes 479240 | tf_op jit(solution)/shard_map/ppermute | solution.py:34
  19.6 3.4 %collective-permute-done.1 = bf16[104,768]{1,0:T(8,128)(2,1)S(1)} collective-permute-done((bf16[104,768]{1,0:T(8,128)(2,1)S(1)}, bf16[104,768]{1,0:T(8,128)(2,1)S(1)}, u32[]{:S(2)}, u32[]{:S(2)}) %collective-permute-start.1) | collective-permute-done | bytes 159776 | tf_op jit(solution)/shard_map/ppermute | solution.py:34
  31.4 9.1 %collective-permute-done.15 = bf16[104,1536]{1,0:T(8,128)(2,1)S(1)} collective-permute-done((bf16[104,1536]{1,0:T(8,128)(2,1)S(1)}, bf16[104,1536]{1,0:T(8,128)(2,1)S(1)}, u32[]{:S(2)}, u32[]{:S(2)}) %collective-permute-start.15) | collective-permute-done | bytes 319520 | tf_op jit(solution)/shard_map/ppermute | solution.py:34
  40.5 11.5 %collective-permute-start.13 = (bf16[104,1536]{1,0:T(8,128)(2,1)S(1)}, bf16[104,1536]{1,0:T(8,128)(2,1)S(1)}, u32[]{:S(2)}, u32[]{:S(2)}) collective-permute-start(bf16[104,1536]{1,0:T(8,128)(2,1)S(1)} %pad_maximum_fusion.5), channel_id=1, source_target_pairs={{0,1},{1,0},{2,3},{3,2},{4,5},{5,4},{6,7},{7,6},{8,9},{9,8},{10,11... | collective-permute-start | bytes 958472 | tf_op jit(solution)/shard_map/ppermute | solution.py:34
  52.0 3.7 %collective-permute-done.14 = bf16[104,1536]{1,0:T(8,128)(2,1)S(1)} collective-permute-done((bf16[104,1536]{1,0:T(8,128)(2,1)S(1)}, bf16[104,1536]{1,0:T(8,128)(2,1)S(1)}, u32[]{:S(2)}, u32[]{:S(2)}) %collective-permute-start.14) | collective-permute-done | bytes 319520 | tf_op jit(solution)/shard_map/ppermute | solution.py:34
  56.8 3.7 %collective-permute-done.13 = bf16[104,1536]{1,0:T(8,128)(2,1)S(1)} collective-permute-done((bf16[104,1536]{1,0:T(8,128)(2,1)S(1)}, bf16[104,1536]{1,0:T(8,128)(2,1)S(1)}, u32[]{:S(2)}, u32[]{:S(2)}) %collective-permute-start.13) | collective-permute-done | bytes 319520 | tf_op jit(solution)/shard_map/ppermute | solution.py:34
  60.7 3.3 %collective-permute-start.17 = (bf16[128,768]{1,0:T(8,128)(2,1)S(1)}, bf16[128,768]{1,0:T(8,128)(2,1)S(1)}, u32[]{:S(2)}, u32[]{:S(2)}) collective-permute-start(bf16[128,768]{1,0:T(8,128)(2,1)S(1)} %get-tuple-element.134), channel_id=1, source_target_pairs={{0,2},{1,3},{2,0},{3,1},{4,6},{5,7},{6,4},{7,5},{8,10},{9,11},{10,... | collective-permute-start | bytes 589832 | tf_op jit(solution)/shard_map/ppermute | solution.py:34
  73.5 4.8 %collective-permute-done.17.refs_2_ = bf16[128,768]{1,0:T(8,128)(2,1)S(1)} collective-permute-done((bf16[128,768]{1,0:T(8,128)(2,1)S(1)}, bf16[128,768]{1,0:T(8,128)(2,1)S(1)}, u32[]{:S(2)}, u32[]{:S(2)}) %collective-permute-start.17) | collective-permute-done | bytes 196640 | tf_op jit(solution)/shard_map/ppermute | solution.py:34
  83.3 7.4 %project.1 = (bf16[512,768]{1,0:T(8,128)(2,1)}, bf16[512,2304]{1,0:T(8,128)(2,1)}, bf16[512,1536]{1,0:T(8,128)(2,1)}) custom-call(s32[8]{0:T(128)} %stack.122.table, bf16[128,768]{1,0:T(8,128)(2,1)} %get-tuple-element.145.refs_0_, bf16[128,768]{1,0:T(8,128)(2,1)} %copy-done.26, bf16[128,768]{1,0:T(8,128)(2,1)} %copy-done.27, bf16[128,768]{1,0:T(8,128)(2,1)} %copy-done.28, ...), custom_call_target="tpu_custom_call" | custom-call | flops 2310000128 | bytes 210000 | tf_op jit(solution)/shard_map/project/pallas_call | solution.py:301
  90.8 10.5 %collective-permute-done.20.refs_6_.refs_22_ = bf16[104,6144]{1,0:T(8,128)(2,1)} collective-permute-done((bf16[104,6144]{1,0:T(8,128)(2,1)}, bf16[104,6144]{1,0:T(8,128)(2,1)}, u32[]{:S(2)}, u32[]{:S(2)}) %collective-permute-start.20) | collective-permute-done | bytes 1277984 | tf_op jit(solution)/shard_map/ppermute | solution.py:39
  106.4 14.6 %attend.1 = (bf16[512,768]{1,0:T(8,128)(2,1)}, f32[512,768]{1,0:T(8,128)}) custom-call(bf16[512,2304]{1,0:T(8,128)(2,1)} %get-tuple-element.158.q_ref.k_ref.v_ref, bf16[512,2304]{1,0:T(8,128)(2,1)} %get-tuple-element.158.q_ref.k_ref.v_ref, bf16[512,2304]{1,0:T(8,128)(2,1)} %get-tuple-element.158.q_ref.k_ref.v_ref, bf16[512,1536]{1,0:T(8,128)(2,1)} %copy-done, ...), custom_call_target="tpu_custom_call" | custom-call | flops 4950000128 | bytes 450000 | tf_op jit(solution)/shard_map/attend/pallas_call | solution.py:347
  122.2 3.0 collective-permute-done.29.refs_11_.refs_27_
  126.2 33.1 %feed.1 = (f32[8,3840]{1,0:T(8,128)}, bf16[512,768]{1,0:T(8,128)(2,1)}, f32[512,768]{1,0:T(8,128)}, bf16[512,768]{1,0:T(8,128)(2,1)}, bf16[4,96,3072]{2,1,0:T(8,...) custom-call(s32[8]{0:T(128)} %stack.122.table, ...), custom_call_target="tpu_custom_call" | custom-call | flops 10890000384 | bytes 990000 | tf_op jit(solution)/shard_map/feed/pallas_call | solution.py:301
  163.5 10.4 %attend_back.2 = (bf16[512,384]{1,0:T(8,128)(2,1)}, f32[512,768]{1,0:T(8,128)}, bf16[512,768]{1,0:T(8,128)(2,1)}) custom-call(bf16[512,2304]{1,0:T(8,128)(2,1)} %get-tuple-element.158.q_ref.k_ref.v_ref, bf16[512,2304]{1,0:T(8,128)(2,1)} %get-tuple-element.158.q_ref.k_ref.v_ref, bf16[512,2304]{1,0:T(8,128)(2,1)} %get-tuple-element.158.q_ref.k_ref.v_ref, ...), custom_call_target="tpu_custom_call" | custom-call | flops 2969999872 | bytes 270000 | tf_op jit(solution)/shard_map/attend_back/pallas_call | solution.py:410
  184.3 10.4 %attend_back.3 = (bf16[512,384]{1,0:T(8,128)(2,1)}, f32[512,768]{1,0:T(8,128)}, bf16[512,768]{1,0:T(8,128)(2,1)}) custom-call(bf16[512,2304]{1,0:T(8,128)(2,1)} %get-tuple-element.158.q_ref.k_ref.v_ref, bf16[512,2304]{1,0:T(8,128)(2,1)} %get-tuple-element.158.q_ref.k_ref.v_ref, bf16[512,2304]{1,0:T(8,128)(2,1)} %get-tuple-element.158.q_ref.k_ref.v_ref, ...), custom_call_target="tpu_custom_call" | custom-call | flops 2969999872 | bytes 270000 | tf_op jit(solution)/shard_map/attend_back/pallas_call | solution.py:410
  197.4 8.7 %project_back.1 = (bf16[512,768]{1,0:T(8,128)(2,1)}, bf16[512,2304]{1,0:T(8,128)(2,1)}) custom-call(s32[8]{0:T(128)} %stack.122.table, f32[512,768]{1,0:T(8,128)} %get-tuple-element.178.da_ref, bf16[512,384]{1,0:T(8,128)(2,1)} %get-tuple-element.181.refs_0_, f32[512,768]{1,0:T(8,128)} %get-tuple-element.182.refs_1_, ...), custom_call_target="tpu_custom_call" | custom-call | flops 2969999872 | bytes 270000 | tf_op jit(solution)/shard_map/project_back/pallas_call | solution.py:301
  206.1 7.6 %collective-permute-done.37 = bf16[2,96,3072]{2,1,0:T(8,128)(2,1)} collective-permute-done((bf16[2,96,3072]{2,1,0:T(8,128)(2,1)}, bf16[2,96,3072]{2,1,0:T(8,128)(2,1)}, u32[]{:S(2)}, u32[]{:S(2)}) %collective-permute-start.37) | collective-permute-done | bytes 1179680 | tf_op jit(solution)/shard_map/ppermute | solution.py:39
  227.2 6.8 %project_grads.1 = (f32[8,2304]{1,0:T(8,128)}, bf16[4,104,2304]{2,1,0:T(8,128)(2,1)}, bf16[4,104,2304]{2,1,0:T(8,128)(2,1)}) custom-call(s32[8]{0:T(128)} %stack.122.table, bf16[512,768]{1,0:T(8,128)(2,1)} %get-tuple-element.157.x_ref, bf16[512,2304]{1,0:T(8,128)(2,1)} %get-tuple-element.206.dqkv_ref), custom_call_target="tpu_custom_call" | custom-call | flops 2310000128 | bytes 210000 | tf_op jit(solution)/shard_map/project_grads/pallas_call | solution.py:301
  234.0 6.6 %collective-permute-done.42 = bf16[128,768]{1,0:T(8,128)(2,1)} collective-permute-done((bf16[128,768]{1,0:T(8,128)(2,1)}, bf16[128,768]{1,0:T(8,128)(2,1)}, u32[]{:S(2)}, u32[]{:S(2)}) %collective-permute-start.42) | collective-permute-done | bytes 196640 | tf_op jit(solution)/shard_map/ppermute | solution.py:34
  255.3 5.9 %collective-permute-done.46 = bf16[96,768]{1,0:T(8,128)(2,1)S(1)} collective-permute-done((bf16[96,768]{1,0:T(8,128)(2,1)S(1)}, bf16[96,768]{1,0:T(8,128)(2,1)S(1)}, u32[]{:S(2)}, u32[]{:S(2)}) %collective-permute-start.46) | collective-permute-done | bytes 147488 | tf_op jit(solution)/shard_map/ppermute | solution.py:34
  261.5 10.9 %collective-permute-done.47 = bf16[96,768]{1,0:T(8,128)(2,1)S(1)} collective-permute-done((bf16[96,768]{1,0:T(8,128)(2,1)S(1)}, bf16[96,768]{1,0:T(8,128)(2,1)S(1)}, u32[]{:S(2)}, u32[]{:S(2)}) %collective-permute-start.47) | collective-permute-done | bytes 147488 | tf_op jit(solution)/shard_map/ppermute | solution.py:34
  277.1 5.3 %collective-permute-done.51 = bf16[104,960]{1,0:T(8,128)(2,1)S(1)} collective-permute-done((bf16[104,960]{1,0:T(8,128)(2,1)S(1)}, bf16[104,960]{1,0:T(8,128)(2,1)S(1)}, u32[]{:S(2)}, u32[]{:S(2)}) %collective-permute-start.51) | collective-permute-done | bytes 199712 | tf_op jit(solution)/shard_map/ppermute | solution.py:34
  286.3 3.0 collective-permute-start.56
  293.7 5.7 %collective-permute-done.56 = bf16[104,576]{1,0:T(8,128)(2,1)S(1)} collective-permute-done((bf16[104,576]{1,0:T(8,128)(2,1)S(1)}, bf16[104,576]{1,0:T(8,128)(2,1)S(1)}, u32[]{:S(2)}, u32[]{:S(2)}) %collective-permute-start.56) | collective-permute-done | bytes 119840 | tf_op jit(solution)/shard_map/ppermute | solution.py:34
  (266 shorter events, 105.2 us)
Async XLA Ops:
  24.0 31.7 %collective-permute-start.8 = (bf16[104,3072]{1,0:T(8,128)(2,1)S(1)}, bf16[104,3072]{1,0:T(8,128)(2,1)}, u32[]{:S(2)}, u32[]{:S(2)}) collective-permute-start(bf16[104,3072]{1,0:T(8,128)(2,1)S(1)} %maximum_maximum_fusion.refs_5_.refs_12_.refs_6_), channel_id=1, source_target_pairs={{0,24},{4,28},{8,16},{12,20},{16,8},{20,12},{24,0},{28,4},{1,25},{... | collective-permute-start | bytes 1916936 | tf_op jit(solution)/shard_map/ppermute | solution.py:39
  26.5 29.7 %collective-permute-start.7 = (bf16[104,3072]{1,0:T(8,128)(2,1)S(1)}, bf16[104,3072]{1,0:T(8,128)(2,1)}, u32[]{:S(2)}, u32[]{:S(2)}) collective-permute-start(bf16[104,3072]{1,0:T(8,128)(2,1)S(1)} %maximum_maximum_fusion.refs_5_.refs_12_.refs_6_), channel_id=1, source_target_pairs={{0,16},{4,12},{8,24},{12,4},{16,0},{20,28},{24,8},{28,20},{1,17},{... | collective-permute-start | bytes 1916936 | tf_op jit(solution)/shard_map/ppermute | solution.py:39
  27.0 29.3 %collective-permute-start.6 = (bf16[104,3072]{1,0:T(8,128)(2,1)S(1)}, bf16[104,3072]{1,0:T(8,128)(2,1)}, u32[]{:S(2)}, u32[]{:S(2)}) collective-permute-start(bf16[104,3072]{1,0:T(8,128)(2,1)S(1)} %maximum_maximum_fusion.refs_5_.refs_12_.refs_6_), channel_id=1, source_target_pairs={{0,8},{4,20},{8,0},{12,28},{16,24},{20,4},{24,16},{28,12},{1,9},{5... | collective-permute-start | bytes 1916936 | tf_op jit(solution)/shard_map/ppermute | solution.py:39
  30.7 25.0 %collective-permute-start.14 = (bf16[104,1536]{1,0:T(8,128)(2,1)S(1)}, bf16[104,1536]{1,0:T(8,128)(2,1)S(1)}, u32[]{:S(2)}, u32[]{:S(2)}) collective-permute-start(bf16[104,1536]{1,0:T(8,128)(2,1)S(1)} %pad_maximum_fusion.5), channel_id=1, source_target_pairs={{0,2},{1,3},{2,0},{3,1},{4,6},{5,7},{6,4},{7,5},{8,10},{9,11},{10,... | collective-permute-start | bytes 958472 | tf_op jit(solution)/shard_map/ppermute | solution.py:34
  40.5 20.0 %collective-permute-start.13 = (bf16[104,1536]{1,0:T(8,128)(2,1)S(1)}, bf16[104,1536]{1,0:T(8,128)(2,1)S(1)}, u32[]{:S(2)}, u32[]{:S(2)}) collective-permute-start(bf16[104,1536]{1,0:T(8,128)(2,1)S(1)} %pad_maximum_fusion.5), channel_id=1, source_target_pairs={{0,1},{1,0},{2,3},{3,2},{4,5},{5,4},{6,7},{7,6},{8,9},{9,8},{10,11... | collective-permute-start | bytes 958472 | tf_op jit(solution)/shard_map/ppermute | solution.py:34
  60.7 17.6 %collective-permute-start.17 = (bf16[128,768]{1,0:T(8,128)(2,1)S(1)}, bf16[128,768]{1,0:T(8,128)(2,1)S(1)}, u32[]{:S(2)}, u32[]{:S(2)}) collective-permute-start(bf16[128,768]{1,0:T(8,128)(2,1)S(1)} %get-tuple-element.134), channel_id=1, source_target_pairs={{0,2},{1,3},{2,0},{3,1},{4,6},{5,7},{6,4},{7,5},{8,10},{9,11},{10,... | collective-permute-start | bytes 589832 | tf_op jit(solution)/shard_map/ppermute | solution.py:34
  70.7 30.6 %collective-permute-start.20 = (bf16[104,6144]{1,0:T(8,128)(2,1)}, bf16[104,6144]{1,0:T(8,128)(2,1)}, u32[]{:S(2)}, u32[]{:S(2)}) collective-permute-start(bf16[104,6144]{1,0:T(8,128)(2,1)} %constant_dynamic-update-slice_fusion.refs_4_.refs_20_), channel_id=1, source_target_pairs={{0,16},{4,12},{8,24},{12,4},{16,0},{20,28},{24,8},{28,20},{1,17},{... | collective-permute-start | bytes 3833864 | tf_op jit(solution)/shard_map/ppermute | solution.py:39
  72.0 29.3 %collective-permute-start.19 = (bf16[104,6144]{1,0:T(8,128)(2,1)}, bf16[104,6144]{1,0:T(8,128)(2,1)}, u32[]{:S(2)}, u32[]{:S(2)}) collective-permute-start(bf16[104,6144]{1,0:T(8,128)(2,1)} %constant_dynamic-update-slice_fusion.refs_4_.refs_20_), channel_id=1, source_target_pairs={{0,8},{4,20},{8,0},{12,28},{16,24},{20,4},{24,16},{28,12},{1,9},{5... | collective-permute-start | bytes 3833864 | tf_op jit(solution)/shard_map/ppermute | solution.py:39
  78.3 23.0 %collective-permute-start.22 = (bf16[104,6144]{1,0:T(8,128)(2,1)}, bf16[104,6144]{1,0:T(8,128)(2,1)}, u32[]{:S(2)}, u32[]{:S(2)}) collective-permute-start(bf16[104,6144]{1,0:T(8,128)(2,1)} %constant_dynamic-update-slice_fusion.refs_4_.refs_20_), channel_id=1, source_target_pairs={{0,4},{4,0},{8,12},{12,8},{16,20},{20,16},{24,28},{28,24},{1,5},{5... | collective-permute-start | bytes 3833864 | tf_op jit(solution)/shard_map/ppermute | solution.py:39
  101.3 19.7 %collective-permute-start.26 = (bf16[104,6144]{1,0:T(8,128)(2,1)}, bf16[104,6144]{1,0:T(8,128)(2,1)S(1)}, u32[]{:S(2)}, u32[]{:S(2)}) collective-permute-start(bf16[104,6144]{1,0:T(8,128)(2,1)} %collective-permute-done.20.refs_6_.refs_22_), channel_id=1, source_target_pairs={{0,4},{4,0},{8,12},{12,8},{16,20},{20,16},{24,28},{28,24},{1,5},{5... | collective-permute-start | bytes 3833864 | tf_op jit(solution)/shard_map/ppermute | solution.py:39
  101.8 19.2 %collective-permute-start.25 = (bf16[104,6144]{1,0:T(8,128)(2,1)}, bf16[104,6144]{1,0:T(8,128)(2,1)S(1)}, u32[]{:S(2)}, u32[]{:S(2)}) collective-permute-start(bf16[104,6144]{1,0:T(8,128)(2,1)} %collective-permute-done.19.refs_5_.refs_21_), channel_id=1, source_target_pairs={{0,4},{4,0},{8,12},{12,8},{16,20},{20,16},{24,28},{28,24},{1,5},{5... | collective-permute-start | bytes 3833864 | tf_op jit(solution)/shard_map/ppermute | solution.py:39
  101.9 19.2 %collective-permute-start.24 = (bf16[104,6144]{1,0:T(8,128)(2,1)}, bf16[104,6144]{1,0:T(8,128)(2,1)S(1)}, u32[]{:S(2)}, u32[]{:S(2)}) collective-permute-start(bf16[104,6144]{1,0:T(8,128)(2,1)} %collective-permute-done.19.refs_5_.refs_21_), channel_id=1, source_target_pairs={{0,16},{4,12},{8,24},{12,4},{16,0},{20,28},{24,8},{28,20},{1,17},{... | collective-permute-start | bytes 3833864 | tf_op jit(solution)/shard_map/ppermute | solution.py:39
  103.4 17.6 %collective-permute-start.28 = (bf16[128,768]{1,0:T(8,128)(2,1)S(1)}, bf16[128,768]{1,0:T(8,128)(2,1)S(1)}, u32[]{:S(2)}, u32[]{:S(2)}) collective-permute-start(bf16[128,768]{1,0:T(8,128)(2,1)S(1)} %get-tuple-element.286), channel_id=1, source_target_pairs={{0,2},{1,3},{2,0},{3,1},{4,6},{5,7},{6,4},{7,5},{8,10},{9,11},{10,... | collective-permute-start | bytes 589832 | tf_op jit(solution)/shard_map/ppermute | solution.py:34
  173.9 20.9 %collective-permute-start.33 = (bf16[512,768]{1,0:T(8,128)(2,1)}, bf16[512,768]{1,0:T(8,128)(2,1)}, u32[]{:S(2)}, u32[]{:S(2)}) collective-permute-start(bf16[512,768]{1,0:T(8,128)(2,1)} %get-tuple-element.194), channel_id=1, source_target_pairs={{0,4},{4,0},{8,12},{12,8},{16,20},{20,16},{24,28},{28,24},{1,5},{5... | collective-permute-start | bytes 2359304 | tf_op jit(solution)/shard_map/ppermute | solution.py:39
  180.0 33.6 %collective-permute-start.38 = (bf16[2,104,3840]{2,1,0:T(8,128)(2,1)}, bf16[2,104,3840]{2,1,0:T(8,128)(2,1)}, u32[]{:S(2)}, u32[]{:S(2)}) collective-permute-start(bf16[2,104,3840]{2,1,0:T(8,128)(2,1)} %add_convert_fusion), channel_id=1, source_target_pairs={{0,16},{4,12},{8,24},{12,4},{16,0},{20,28},{24,8},{28,20},{1,17},{... | collective-permute-start | bytes 4792328 | tf_op jit(solution)/shard_map/ppermute | solution.py:39
  183.6 30.1 %collective-permute-start.37 = (bf16[2,96,3072]{2,1,0:T(8,128)(2,1)}, bf16[2,96,3072]{2,1,0:T(8,128)(2,1)}, u32[]{:S(2)}, u32[]{:S(2)}) collective-permute-start(bf16[2,96,3072]{2,1,0:T(8,128)(2,1)} %add_convert_fusion.1), channel_id=1, source_target_pairs={{0,16},{4,12},{8,24},{12,4},{16,0},{20,28},{24,8},{28,20},{1,17},{... | collective-permute-start | bytes 3538952 | tf_op jit(solution)/shard_map/ppermute | solution.py:39
  218.7 21.9 %collective-permute-start.40 = (bf16[1,104,3840]{2,1,0:T(8,128)(2,1)}, bf16[1,104,3840]{2,1,0:T(8,128)(2,1)}, u32[]{:S(2)}, u32[]{:S(2)}) collective-permute-start(bf16[1,104,3840]{2,1,0:T(8,128)(2,1)} %add_convert_fusion.3), channel_id=1, source_target_pairs={{0,8},{4,20},{8,0},{12,28},{16,24},{20,4},{24,16},{28,12},{1,9},{5... | collective-permute-start | bytes 2396168 | tf_op jit(solution)/shard_map/ppermute | solution.py:39
  219.1 21.5 %collective-permute-start.39 = (bf16[1,96,3072]{2,1,0:T(8,128)(2,1)}, bf16[1,96,3072]{2,1,0:T(8,128)(2,1)}, u32[]{:S(2)}, u32[]{:S(2)}) collective-permute-start(bf16[1,96,3072]{2,1,0:T(8,128)(2,1)} %add_convert_fusion.4), channel_id=1, source_target_pairs={{0,8},{4,20},{8,0},{12,28},{16,24},{20,4},{24,16},{28,12},{1,9},{5... | collective-permute-start | bytes 1769480 | tf_op jit(solution)/shard_map/ppermute | solution.py:39
  224.4 16.2 %collective-permute-start.42 = (bf16[128,768]{1,0:T(8,128)(2,1)}, bf16[128,768]{1,0:T(8,128)(2,1)}, u32[]{:S(2)}, u32[]{:S(2)}) collective-permute-start(bf16[128,768]{1,0:T(8,128)(2,1)} %get-tuple-element.279), channel_id=1, source_target_pairs={{0,2},{1,3},{2,0},{3,1},{4,6},{5,7},{6,4},{7,5},{8,10},{9,11},{10,... | collective-permute-start | bytes 589832 | tf_op jit(solution)/shard_map/ppermute | solution.py:34
  246.8 27.1 %collective-permute-start.45 = (bf16[2,104,2304]{2,1,0:T(8,128)(2,1)S(1)}, bf16[2,104,2304]{2,1,0:T(8,128)(2,1)S(1)}, u32[]{:S(2)}, u32[]{:S(2)}) collective-permute-start(bf16[2,104,2304]{2,1,0:T(8,128)(2,1)S(1)} %add_convert_fusion.2), channel_id=1, source_target_pairs={{0,16},{4,12},{8,24},{12,4},{16,0},{20,28},{24,8},{28,20},{1,17},{... | collective-permute-start | bytes 2875400 | tf_op jit(solution)/shard_map/ppermute | solution.py:39
  248.5 28.6 %collective-permute-start.50 = (bf16[104,960]{1,0:T(8,128)(2,1)S(1)}, bf16[104,960]{1,0:T(8,128)(2,1)S(1)}, u32[]{:S(2)}, u32[]{:S(2)}) collective-permute-start(bf16[104,960]{1,0:T(8,128)(2,1)S(1)} %pad_maximum_fusion.7), channel_id=1, source_target_pairs={{0,1},{1,0},{2,3},{3,2},{4,5},{5,4},{6,7},{7,6},{8,9},{9,8},{10,11... | collective-permute-start | bytes 599048 | tf_op jit(solution)/shard_map/ppermute | solution.py:34
  251.9 20.5 %collective-permute-start.47 = (bf16[96,768]{1,0:T(8,128)(2,1)S(1)}, bf16[96,768]{1,0:T(8,128)(2,1)S(1)}, u32[]{:S(2)}, u32[]{:S(2)}) collective-permute-start(bf16[96,768]{1,0:T(8,128)(2,1)S(1)} %get-tuple-element.217), channel_id=1, source_target_pairs={{0,2},{1,3},{2,0},{3,1},{4,6},{5,7},{6,4},{7,5},{8,10},{9,11},{10,... | collective-permute-start | bytes 442376 | tf_op jit(solution)/shard_map/ppermute | solution.py:34
  252.0 21.9 %collective-permute-start.48 = (bf16[96,768]{1,0:T(8,128)(2,1)S(1)}, bf16[96,768]{1,0:T(8,128)(2,1)S(1)}, u32[]{:S(2)}, u32[]{:S(2)}) collective-permute-start(bf16[96,768]{1,0:T(8,128)(2,1)S(1)} %get-tuple-element.218), channel_id=1, source_target_pairs={{0,3},{1,2},{2,1},{3,0},{4,7},{5,6},{6,5},{7,4},{8,11},{9,10},{10,... | collective-permute-start | bytes 442376 | tf_op jit(solution)/shard_map/ppermute | solution.py:34
  261.2 21.2 %collective-permute-start.51 = (bf16[104,960]{1,0:T(8,128)(2,1)S(1)}, bf16[104,960]{1,0:T(8,128)(2,1)S(1)}, u32[]{:S(2)}, u32[]{:S(2)}) collective-permute-start(bf16[104,960]{1,0:T(8,128)(2,1)S(1)} %pad_maximum_fusion.8), channel_id=1, source_target_pairs={{0,2},{1,3},{2,0},{3,1},{4,6},{5,7},{6,4},{7,5},{8,10},{9,11},{10,... | collective-permute-start | bytes 599048 | tf_op jit(solution)/shard_map/ppermute | solution.py:34
  (67 other events, 658.6 us)
where the time goes:
time: 303 us; the launch traced here: 302 us
  Pallas kernels  91.4 us (30%)
  waiting for transfers between devices  86 us (28%)
  starting transfers between devices  65.8 us (22%)
  other arithmetic  28.3 us (9%)
  local copies, waits for them, and re-layouts  28.2 us (9%)
    ppermute x27, waiting for transfers between devices, mp_swap(): return lax.ppermute(value, 'mp', [(i, i ^ step) for i in range(N_MP)])  59.3 us
    pallas_call x4, Pallas kernels, call(): pl.pallas_call(body, out_shape=tuple(outs), in_specs=[pl.BlockSpec(memory...  56.1 us
    ppermute x27, starting transfers between devices, mp_swap(): return lax.ppermute(value, 'mp', [(i, i ^ step) for i in range(N_MP)])  48.5 us
    ppermute x31, waiting for transfers between devices, dp_swap(): return lax.ppermute(value, 'dp', [(i, target(i)) for i in range(size)])  26.7 us
    pallas_call x2, Pallas kernels, attend_back(): pl.pallas_call(attend_back_kernel, out_shape=(jax.ShapeDtypeStruct((rows,...  20.8 us
    ppermute x31, starting transfers between devices, dp_swap(): return lax.ppermute(value, 'dp', [(i, target(i)) for i in range(size)])  17.3 us
    pallas_call x1, Pallas kernels, attend(): pl.pallas_call(attend_kernel, out_shape=(jax.ShapeDtypeStruct((rows, widt...  14.6 us
    unnamed x73, local copies, waits for them, and re-layouts  13.2 us
  transfers between devices with their start and end apart: 58, of which 19 were waited for; matrix products, arithmetic and copies ran while one was open for 12% of the time, Pallas kernels for 19%

commit v1 on v0

--- a/solution.py
+++ b/solution.py
@@ -567,14 +567,15 @@
         up_w.whole()
         down_w.whole()
 
-        @pl.loop(0, count)
-        def _(t):
-            at = pl.multiple_of(t * tile, tile)
-            u = dot(h_ref[...], up_w.at(at), NN)
-            act, slope = gelu_parts(u + up_b_ref[:, pl.ds(at, tile)])
-            act_ref[:, pl.ds(at, tile)] = act.astype(BF16)
-            slope_ref[:, pl.ds(at, tile)] = slope.astype(BF16)
-            dz_ref[...] += dot(act_ref[:, pl.ds(at, tile)], down_w.at(at), NT)
+        @pl.loop(0, count // 2)
+        def _(i):
+            ats = [pl.multiple_of((2 * i + k) * tile, tile) for k in range(2)]
+            us = [dot(h_ref[...], up_w.at(at), NN) for at in ats]
+            for at, u in zip(ats, us):
+                act, slope = gelu_parts(u + up_b_ref[:, pl.ds(at, tile)])
+                act_ref[:, pl.ds(at, tile)] = act.astype(BF16)
+                slope_ref[:, pl.ds(at, tile)] = slope.astype(BF16)
+                dz_ref[...] += dot(act_ref[:, pl.ds(at, tile)], down_w.at(at), NT)
 
         feed = dz_ref[...]
         h = n1_ref[...] * row(1) + row(2)
@@ -931,8 +932,8 @@
         b_mid = dp_swap(a_mid, early)
     attn_shared, *g_attn = project_grads(x, dqkv, table, attn_p)
     if fast:
-        both = tie(*g_attn, b_down, b_mid, *grad_parts)
-        g_attn, b_down, b_mid, grad_parts = both[:2], both[2], both[3], both[4:]
+        both = tie(*g_attn, b_down, b_mid, grad_parts[3])
+        g_attn, b_down, b_mid, grad_parts[3] = both[:2], both[2], both[3], both[4]
         b_attn = core_swap(g_attn[1])
         s_down = by_group_of(last_sum(stays(t_down, b_down)), [units])
         t_attn = [g_attn[0], b_attn]

time: 303 us -> 304 us (level)
  starting transfers between devices: 65.8 us -> 73.4 us
  waiting for transfers between devices: 86 us -> 79.1 us
    ppermute x27, starting transfers between devices: 48.5 us -> 55.8 us  [mp_swap(): return lax.ppermute(value, 'mp', [(i, i ^ step) for i in range(N_MP)])]
    ppermute x27, waiting for transfers between devices: 59.3 us -> 52.8 us  [mp_swap(): return lax.ppermute(value, 'mp', [(i, i ^ step) for i in range(N_MP)])]
  transfers between devices with their start and end apart: 58 -> 58, of which waited for: 19 -> 20; matrix products, arithmetic and copies ran while one was open for 12% -> 12% of each run, Pallas kernels for 19% -> 19%
where the time goes in v1:
time: 304 us; the launch traced here: 303 us
  Pallas kernels  91.3 us (30%)
  waiting for transfers between devices  79.1 us (26%)
  starting transfers between devices  73.4 us (24%)
  other arithmetic  28.4 us (9%)
  local copies, waits for them, and re-layouts  28.2 us (9%)
    pallas_call x4, Pallas kernels, call(): pl.pallas_call(body, out_shape=tuple(outs), in_specs=[pl.BlockSpec(memory...  55.9 us
    ppermute x27, starting transfers between devices, mp_swap(): return lax.ppermute(value, 'mp', [(i, i ^ step) for i in range(N_MP)])  55.8 us
    ppermute x27, waiting for transfers between devices, mp_swap(): return lax.ppermute(value, 'mp', [(i, i ^ step) for i in range(N_MP)])  52.8 us
    ppermute x31, waiting for transfers between devices, dp_swap(): return lax.ppermute(value, 'dp', [(i, target(i)) for i in range(size)])  26.3 us
    pallas_call x2, Pallas kernels, attend_back(): pl.pallas_call(attend_back_kernel, out_shape=(jax.ShapeDtypeStruct((rows,...  20.8 us
    ppermute x31, starting transfers between devices, dp_swap(): return lax.ppermute(value, 'dp', [(i, target(i)) for i in range(size)])  17.6 us
    pallas_call x1, Pallas kernels, attend(): pl.pallas_call(attend_kernel, out_shape=(jax.ShapeDtypeStruct((rows, widt...  14.6 us
    unnamed x73, local copies, waits for them, and re-layouts  13.2 us
  transfers between devices with their start and end apart: 58, of which 20 were waited for; matrix products, arithmetic and copies ran while one was open for 12% of the time, Pallas kernels for 19%

profile of v1, /device:TPU:0, one launch (start us, length us, event | category | flops | bytes accessed | tf_op | source)
XLA Modules:
  0.0 302.6 jit_solution(14023665772607100811)
XLA Ops:
  4.2 5.1 %collective-permute-start.2 = (bf16[104,768]{1,0:T(8,128)(2,1)S(1)}, bf16[104,768]{1,0:T(8,128)(2,1)S(1)}, u32[]{:S(2)}, u32[]{:S(2)}) collective-permute-start(bf16[104,768]{1,0:T(8,128)(2,1)S(1)} %pad_maximum_fusion.10), channel_id=1, source_target_pairs={{0,3},{1,2},{2,1},{3,0},{4,7},{5,6},{6,5},{7,4},{8,11},{9,10},{10,... | collective-permute-start | bytes 479240 | tf_op jit(solution)/shard_map/ppermute | solution.py:34
  19.6 3.4 %collective-permute-done.1 = bf16[104,768]{1,0:T(8,128)(2,1)S(1)} collective-permute-done((bf16[104,768]{1,0:T(8,128)(2,1)S(1)}, bf16[104,768]{1,0:T(8,128)(2,1)S(1)}, u32[]{:S(2)}, u32[]{:S(2)}) %collective-permute-start.1) | collective-permute-done | bytes 159776 | tf_op jit(solution)/shard_map/ppermute | solution.py:34
  31.4 9.1 %collective-permute-done.15 = bf16[104,1536]{1,0:T(8,128)(2,1)S(1)} collective-permute-done((bf16[104,1536]{1,0:T(8,128)(2,1)S(1)}, bf16[104,1536]{1,0:T(8,128)(2,1)S(1)}, u32[]{:S(2)}, u32[]{:S(2)}) %collective-permute-start.15) | collective-permute-done | bytes 319520 | tf_op jit(solution)/shard_map/ppermute | solution.py:34
  40.5 11.5 %collective-permute-start.13 = (bf16[104,1536]{1,0:T(8,128)(2,1)S(1)}, bf16[104,1536]{1,0:T(8,128)(2,1)S(1)}, u32[]{:S(2)}, u32[]{:S(2)}) collective-permute-start(bf16[104,1536]{1,0:T(8,128)(2,1)S(1)} %pad_maximum_fusion.5), channel_id=1, source_target_pairs={{0,1},{1,0},{2,3},{3,2},{4,5},{5,4},{6,7},{7,6},{8,9},{9,8},{10,11... | collective-permute-start | bytes 958472 | tf_op jit(solution)/shard_map/ppermute | solution.py:34
  52.0 3.7 %collective-permute-done.14 = bf16[104,1536]{1,0:T(8,128)(2,1)S(1)} collective-permute-done((bf16[104,1536]{1,0:T(8,128)(2,1)S(1)}, bf16[104,1536]{1,0:T(8,128)(2,1)S(1)}, u32[]{:S(2)}, u32[]{:S(2)}) %collective-permute-start.14) | collective-permute-done | bytes 319520 | tf_op jit(solution)/shard_map/ppermute | solution.py:34
  56.8 3.7 %collective-permute-done.13 = bf16[104,1536]{1,0:T(8,128)(2,1)S(1)} collective-permute-done((bf16[104,1536]{1,0:T(8,128)(2,1)S(1)}, bf16[104,1536]{1,0:T(8,128)(2,1)S(1)}, u32[]{:S(2)}, u32[]{:S(2)}) %collective-permute-start.13) | collective-permute-done | bytes 319520 | tf_op jit(solution)/shard_map/ppermute | solution.py:34
  60.7 3.3 %collective-permute-start.17 = (bf16[128,768]{1,0:T(8,128)(2,1)S(1)}, bf16[128,768]{1,0:T(8,128)(2,1)S(1)}, u32[]{:S(2)}, u32[]{:S(2)}) collective-permute-start(bf16[128,768]{1,0:T(8,128)(2,1)S(1)} %get-tuple-element.131), channel_id=1, source_target_pairs={{0,2},{1,3},{2,0},{3,1},{4,6},{5,7},{6,4},{7,5},{8,10},{9,11},{10,... | collective-permute-start | bytes 589832 | tf_op jit(solution)/shard_map/ppermute | solution.py:34
  73.5 4.8 %collective-permute-done.17.refs_2_ = bf16[128,768]{1,0:T(8,128)(2,1)S(1)} collective-permute-done((bf16[128,768]{1,0:T(8,128)(2,1)S(1)}, bf16[128,768]{1,0:T(8,128)(2,1)S(1)}, u32[]{:S(2)}, u32[]{:S(2)}) %collective-permute-start.17) | collective-permute-done | bytes 196640 | tf_op jit(solution)/shard_map/ppermute | solution.py:34
  83.3 7.4 %project.1 = (bf16[512,768]{1,0:T(8,128)(2,1)}, bf16[512,2304]{1,0:T(8,128)(2,1)}, bf16[512,1536]{1,0:T(8,128)(2,1)}) custom-call(s32[8]{0:T(128)} %stack.122.table, bf16[128,768]{1,0:T(8,128)(2,1)} %get-tuple-element.142.refs_0_, bf16[128,768]{1,0:T(8,128)(2,1)} %copy-done.26, bf16[128,768]{1,0:T(8,128)(2,1)} %copy-done.27, bf16[128,768]{1,0:T(8,128)(2,1)} %copy-done.28, ...), custom_call_target="tpu_custom_call" | custom-call | flops 2310000128 | bytes 210000 | tf_op jit(solution)/shard_map/project/pallas_call | solution.py:301
  90.8 10.5 %collective-permute-done.20.refs_6_.refs_22_ = bf16[104,6144]{1,0:T(8,128)(2,1)} collective-permute-done((bf16[104,6144]{1,0:T(8,128)(2,1)}, bf16[104,6144]{1,0:T(8,128)(2,1)}, u32[]{:S(2)}, u32[]{:S(2)}) %collective-permute-start.20) | collective-permute-done | bytes 1277984 | tf_op jit(solution)/shard_map/ppermute | solution.py:39
  106.4 14.6 %attend.1 = (bf16[512,768]{1,0:T(8,128)(2,1)}, f32[512,768]{1,0:T(8,128)}) custom-call(bf16[512,2304]{1,0:T(8,128)(2,1)} %get-tuple-element.155.q_ref.k_ref.v_ref, bf16[512,2304]{1,0:T(8,128)(2,1)} %get-tuple-element.155.q_ref.k_ref.v_ref, bf16[512,2304]{1,0:T(8,128)(2,1)} %get-tuple-element.155.q_ref.k_ref.v_ref, bf16[512,1536]{1,0:T(8,128)(2,1)} %copy-done, ...), custom_call_target="tpu_custom_call" | custom-call | flops 4950000128 | bytes 450000 | tf_op jit(solution)/shard_map/attend/pallas_call | solution.py:347
  126.2 33.0 %feed.1 = (f32[8,3840]{1,0:T(8,128)}, bf16[512,768]{1,0:T(8,128)(2,1)}, f32[512,768]{1,0:T(8,128)}, bf16[512,768]{1,0:T(8,128)(2,1)}, bf16[4,96,3072]{2,1,0:T(8,...) custom-call(s32[8]{0:T(128)} %stack.122.table, ...), custom_call_target="tpu_custom_call" | custom-call | flops 10890000384 | bytes 990000 | tf_op jit(solution)/shard_map/feed/pallas_call | solution.py:301
  163.3 10.4 %attend_back.2 = (bf16[512,384]{1,0:T(8,128)(2,1)}, f32[512,768]{1,0:T(8,128)}, bf16[512,768]{1,0:T(8,128)(2,1)}) custom-call(bf16[512,2304]{1,0:T(8,128)(2,1)} %get-tuple-element.155.q_ref.k_ref.v_ref, bf16[512,2304]{1,0:T(8,128)(2,1)} %get-tuple-element.155.q_ref.k_ref.v_ref, bf16[512,2304]{1,0:T(8,128)(2,1)} %get-tuple-element.155.q_ref.k_ref.v_ref, ...), custom_call_target="tpu_custom_call" | custom-call | flops 2969999872 | bytes 270000 | tf_op jit(solution)/shard_map/attend_back/pallas_call | solution.py:410
  184.1 10.4 %attend_back.3 = (bf16[512,384]{1,0:T(8,128)(2,1)}, f32[512,768]{1,0:T(8,128)}, bf16[512,768]{1,0:T(8,128)(2,1)}) custom-call(bf16[512,2304]{1,0:T(8,128)(2,1)} %get-tuple-element.155.q_ref.k_ref.v_ref, bf16[512,2304]{1,0:T(8,128)(2,1)} %get-tuple-element.155.q_ref.k_ref.v_ref, bf16[512,2304]{1,0:T(8,128)(2,1)} %get-tuple-element.155.q_ref.k_ref.v_ref, ...), custom_call_target="tpu_custom_call" | custom-call | flops 2969999872 | bytes 270000 | tf_op jit(solution)/shard_map/attend_back/pallas_call | solution.py:410
  197.3 8.7 %project_back.1 = (bf16[512,768]{1,0:T(8,128)(2,1)}, bf16[512,2304]{1,0:T(8,128)(2,1)}) custom-call(s32[8]{0:T(128)} %stack.122.table, f32[512,768]{1,0:T(8,128)} %get-tuple-element.175.da_ref, bf16[512,384]{1,0:T(8,128)(2,1)} %get-tuple-element.178.refs_0_, f32[512,768]{1,0:T(8,128)} %get-tuple-element.179.refs_1_, ...), custom_call_target="tpu_custom_call" | custom-call | flops 2969999872 | bytes 270000 | tf_op jit(solution)/shard_map/project_back/pallas_call | solution.py:301
  205.9 7.6 %collective-permute-done.37 = bf16[2,96,3072]{2,1,0:T(8,128)(2,1)} collective-permute-done((bf16[2,96,3072]{2,1,0:T(8,128)(2,1)}, bf16[2,96,3072]{2,1,0:T(8,128)(2,1)}, u32[]{:S(2)}, u32[]{:S(2)}) %collective-permute-start.37) | collective-permute-done | bytes 1179680 | tf_op jit(solution)/shard_map/ppermute | solution.py:39
  227.0 6.8 %project_grads.1 = (f32[8,2304]{1,0:T(8,128)}, bf16[4,104,2304]{2,1,0:T(8,128)(2,1)}, bf16[4,104,2304]{2,1,0:T(8,128)(2,1)}) custom-call(s32[8]{0:T(128)} %stack.122.table, bf16[512,768]{1,0:T(8,128)(2,1)} %get-tuple-element.154.x_ref, bf16[512,2304]{1,0:T(8,128)(2,1)} %get-tuple-element.203.dqkv_ref), custom_call_target="tpu_custom_call" | custom-call | flops 2310000128 | bytes 210000 | tf_op jit(solution)/shard_map/project_grads/pallas_call | solution.py:301
  233.8 3.1 %collective-permute-done.41 = bf16[128,768]{1,0:T(8,128)(2,1)} collective-permute-done((bf16[128,768]{1,0:T(8,128)(2,1)}, bf16[128,768]{1,0:T(8,128)(2,1)}, u32[]{:S(2)}, u32[]{:S(2)}) %collective-permute-start.41) | collective-permute-done | bytes 196640 | tf_op jit(solution)/shard_map/ppermute | solution.py:34
  245.2 4.4 %collective-permute-start.48 = (bf16[104,960]{1,0:T(8,128)(2,1)S(1)}, bf16[104,960]{1,0:T(8,128)(2,1)S(1)}, u32[]{:S(2)}, u32[]{:S(2)}) collective-permute-start(bf16[104,960]{1,0:T(8,128)(2,1)S(1)} %pad_maximum_fusion.7), channel_id=1, source_target_pairs={{0,1},{1,0},{2,3},{3,2},{4,5},{5,4},{6,7},{7,6},{8,9},{9,8},{10,11... | collective-permute-start | bytes 599048 | tf_op jit(solution)/shard_map/ppermute | solution.py:34
  256.3 4.1 %collective-permute-done.44 = bf16[96,768]{1,0:T(8,128)(2,1)S(1)} collective-permute-done((bf16[96,768]{1,0:T(8,128)(2,1)S(1)}, bf16[96,768]{1,0:T(8,128)(2,1)S(1)}, u32[]{:S(2)}, u32[]{:S(2)}) %collective-permute-start.44) | collective-permute-done | bytes 147488 | tf_op jit(solution)/shard_map/ppermute | solution.py:34
  263.4 3.7 %collective-permute-done.46 = bf16[96,768]{1,0:T(8,128)(2,1)S(1)} collective-permute-done((bf16[96,768]{1,0:T(8,128)(2,1)S(1)}, bf16[96,768]{1,0:T(8,128)(2,1)S(1)}, u32[]{:S(2)}, u32[]{:S(2)}) %collective-permute-start.46) | collective-permute-done | bytes 147488 | tf_op jit(solution)/shard_map/ppermute | solution.py:34
  270.3 10.0 %collective-permute-done.49 = bf16[104,960]{1,0:T(8,128)(2,1)S(1)} collective-permute-done((bf16[104,960]{1,0:T(8,128)(2,1)S(1)}, bf16[104,960]{1,0:T(8,128)(2,1)S(1)}, u32[]{:S(2)}, u32[]{:S(2)}) %collective-permute-start.49) | collective-permute-done | bytes 199712 | tf_op jit(solution)/shard_map/ppermute | solution.py:34
  283.7 5.8 %collective-permute-start.56 = (bf16[104,576]{1,0:T(8,128)(2,1)S(1)}, bf16[104,576]{1,0:T(8,128)(2,1)S(1)}, u32[]{:S(2)}, u32[]{:S(2)}) collective-permute-start(bf16[104,576]{1,0:T(8,128)(2,1)S(1)} %pad_maximum_fusion.12), channel_id=1, source_target_pairs={{0,2},{1,3},{2,0},{3,1},{4,6},{5,7},{6,4},{7,5},{8,10},{9,11},{10,... | collective-permute-start | bytes 359432 | tf_op jit(solution)/shard_map/ppermute | solution.py:34
  293.5 6.1 %collective-permute-done.56 = bf16[104,576]{1,0:T(8,128)(2,1)S(1)} collective-permute-done((bf16[104,576]{1,0:T(8,128)(2,1)S(1)}, bf16[104,576]{1,0:T(8,128)(2,1)S(1)}, u32[]{:S(2)}, u32[]{:S(2)}) %collective-permute-start.56) | collective-permute-done | bytes 119840 | tf_op jit(solution)/shard_map/ppermute | solution.py:34
  (266 shorter events, 109.2 us)
Async XLA Ops:
  24.0 31.7 %collective-permute-start.8 = (bf16[104,3072]{1,0:T(8,128)(2,1)S(1)}, bf16[104,3072]{1,0:T(8,128)(2,1)}, u32[]{:S(2)}, u32[]{:S(2)}) collective-permute-start(bf16[104,3072]{1,0:T(8,128)(2,1)S(1)} %maximum_maximum_fusion.refs_5_.refs_12_.refs_6_), channel_id=1, source_target_pairs={{0,24},{4,28},{8,16},{12,20},{16,8},{20,12},{24,0},{28,4},{1,25},{... | collective-permute-start | bytes 1916936 | tf_op jit(solution)/shard_map/ppermute | solution.py:39
  26.5 29.7 %collective-permute-start.7 = (bf16[104,3072]{1,0:T(8,128)(2,1)S(1)}, bf16[104,3072]{1,0:T(8,128)(2,1)}, u32[]{:S(2)}, u32[]{:S(2)}) collective-permute-start(bf16[104,3072]{1,0:T(8,128)(2,1)S(1)} %maximum_maximum_fusion.refs_5_.refs_12_.refs_6_), channel_id=1, source_target_pairs={{0,16},{4,12},{8,24},{12,4},{16,0},{20,28},{24,8},{28,20},{1,17},{... | collective-permute-start | bytes 1916936 | tf_op jit(solution)/shard_map/ppermute | solution.py:39
  27.0 29.3 %collective-permute-start.6 = (bf16[104,3072]{1,0:T(8,128)(2,1)S(1)}, bf16[104,3072]{1,0:T(8,128)(2,1)}, u32[]{:S(2)}, u32[]{:S(2)}) collective-permute-start(bf16[104,3072]{1,0:T(8,128)(2,1)S(1)} %maximum_maximum_fusion.refs_5_.refs_12_.refs_6_), channel_id=1, source_target_pairs={{0,8},{4,20},{8,0},{12,28},{16,24},{20,4},{24,16},{28,12},{1,9},{5... | collective-permute-start | bytes 1916936 | tf_op jit(solution)/shard_map/ppermute | solution.py:39
  30.7 25.0 %collective-permute-start.14 = (bf16[104,1536]{1,0:T(8,128)(2,1)S(1)}, bf16[104,1536]{1,0:T(8,128)(2,1)S(1)}, u32[]{:S(2)}, u32[]{:S(2)}) collective-permute-start(bf16[104,1536]{1,0:T(8,128)(2,1)S(1)} %pad_maximum_fusion.5), channel_id=1, source_target_pairs={{0,2},{1,3},{2,0},{3,1},{4,6},{5,7},{6,4},{7,5},{8,10},{9,11},{10,... | collective-permute-start | bytes 958472 | tf_op jit(solution)/shard_map/ppermute | solution.py:34
  40.5 20.0 %collective-permute-start.13 = (bf16[104,1536]{1,0:T(8,128)(2,1)S(1)}, bf16[104,1536]{1,0:T(8,128)(2,1)S(1)}, u32[]{:S(2)}, u32[]{:S(2)}) collective-permute-start(bf16[104,1536]{1,0:T(8,128)(2,1)S(1)} %pad_maximum_fusion.5), channel_id=1, source_target_pairs={{0,1},{1,0},{2,3},{3,2},{4,5},{5,4},{6,7},{7,6},{8,9},{9,8},{10,11... | collective-permute-start | bytes 958472 | tf_op jit(solution)/shard_map/ppermute | solution.py:34
  60.7 17.6 %collective-permute-start.17 = (bf16[128,768]{1,0:T(8,128)(2,1)S(1)}, bf16[128,768]{1,0:T(8,128)(2,1)S(1)}, u32[]{:S(2)}, u32[]{:S(2)}) collective-permute-start(bf16[128,768]{1,0:T(8,128)(2,1)S(1)} %get-tuple-element.131), channel_id=1, source_target_pairs={{0,2},{1,3},{2,0},{3,1},{4,6},{5,7},{6,4},{7,5},{8,10},{9,11},{10,... | collective-permute-start | bytes 589832 | tf_op jit(solution)/shard_map/ppermute | solution.py:34
  70.7 30.6 %collective-permute-start.20 = (bf16[104,6144]{1,0:T(8,128)(2,1)}, bf16[104,6144]{1,0:T(8,128)(2,1)}, u32[]{:S(2)}, u32[]{:S(2)}) collective-permute-start(bf16[104,6144]{1,0:T(8,128)(2,1)} %constant_dynamic-update-slice_fusion.refs_4_.refs_20_), channel_id=1, source_target_pairs={{0,16},{4,12},{8,24},{12,4},{16,0},{20,28},{24,8},{28,20},{1,17},{... | collective-permute-start | bytes 3833864 | tf_op jit(solution)/shard_map/ppermute | solution.py:39
  72.0 29.3 %collective-permute-start.19 = (bf16[104,6144]{1,0:T(8,128)(2,1)}, bf16[104,6144]{1,0:T(8,128)(2,1)}, u32[]{:S(2)}, u32[]{:S(2)}) collective-permute-start(bf16[104,6144]{1,0:T(8,128)(2,1)} %constant_dynamic-update-slice_fusion.refs_4_.refs_20_), channel_id=1, source_target_pairs={{0,8},{4,20},{8,0},{12,28},{16,24},{20,4},{24,16},{28,12},{1,9},{5... | collective-permute-start | bytes 3833864 | tf_op jit(solution)/shard_map/ppermute | solution.py:39
  78.3 23.0 %collective-permute-start.22 = (bf16[104,6144]{1,0:T(8,128)(2,1)}, bf16[104,6144]{1,0:T(8,128)(2,1)}, u32[]{:S(2)}, u32[]{:S(2)}) collective-permute-start(bf16[104,6144]{1,0:T(8,128)(2,1)} %constant_dynamic-update-slice_fusion.refs_4_.refs_20_), channel_id=1, source_target_pairs={{0,4},{4,0},{8,12},{12,8},{16,20},{20,16},{24,28},{28,24},{1,5},{5... | collective-permute-start | bytes 3833864 | tf_op jit(solution)/shard_map/ppermute | solution.py:39
  101.3 19.7 %collective-permute-start.26 = (bf16[104,6144]{1,0:T(8,128)(2,1)}, bf16[104,6144]{1,0:T(8,128)(2,1)S(1)}, u32[]{:S(2)}, u32[]{:S(2)}) collective-permute-start(bf16[104,6144]{1,0:T(8,128)(2,1)} %collective-permute-done.20.refs_6_.refs_22_), channel_id=1, source_target_pairs={{0,4},{4,0},{8,12},{12,8},{16,20},{20,16},{24,28},{28,24},{1,5},{5... | collective-permute-start | bytes 3833864 | tf_op jit(solution)/shard_map/ppermute | solution.py:39
  101.8 19.2 %collective-permute-start.25 = (bf16[104,6144]{1,0:T(8,128)(2,1)}, bf16[104,6144]{1,0:T(8,128)(2,1)S(1)}, u32[]{:S(2)}, u32[]{:S(2)}) collective-permute-start(bf16[104,6144]{1,0:T(8,128)(2,1)} %collective-permute-done.19.refs_5_.refs_21_), channel_id=1, source_target_pairs={{0,4},{4,0},{8,12},{12,8},{16,20},{20,16},{24,28},{28,24},{1,5},{5... | collective-permute-start | bytes 3833864 | tf_op jit(solution)/shard_map/ppermute | solution.py:39
  101.9 19.2 %collective-permute-start.24 = (bf16[104,6144]{1,0:T(8,128)(2,1)}, bf16[104,6144]{1,0:T(8,128)(2,1)S(1)}, u32[]{:S(2)}, u32[]{:S(2)}) collective-permute-start(bf16[104,6144]{1,0:T(8,128)(2,1)} %collective-permute-done.19.refs_5_.refs_21_), channel_id=1, source_target_pairs={{0,16},{4,12},{8,24},{12,4},{16,0},{20,28},{24,8},{28,20},{1,17},{... | collective-permute-start | bytes 3833864 | tf_op jit(solution)/shard_map/ppermute | solution.py:39
  103.4 17.6 %collective-permute-start.28 = (bf16[128,768]{1,0:T(8,128)(2,1)S(1)}, bf16[128,768]{1,0:T(8,128)(2,1)S(1)}, u32[]{:S(2)}, u32[]{:S(2)}) collective-permute-start(bf16[128,768]{1,0:T(8,128)(2,1)S(1)} %get-tuple-element.280), channel_id=1, source_target_pairs={{0,2},{1,3},{2,0},{3,1},{4,6},{5,7},{6,4},{7,5},{8,10},{9,11},{10,... | collective-permute-start | bytes 589832 | tf_op jit(solution)/shard_map/ppermute | solution.py:34
  173.7 20.9 %collective-permute-start.33 = (bf16[512,768]{1,0:T(8,128)(2,1)}, bf16[512,768]{1,0:T(8,128)(2,1)}, u32[]{:S(2)}, u32[]{:S(2)}) collective-permute-start(bf16[512,768]{1,0:T(8,128)(2,1)} %get-tuple-element.191), channel_id=1, source_target_pairs={{0,4},{4,0},{8,12},{12,8},{16,20},{20,16},{24,28},{28,24},{1,5},{5... | collective-permute-start | bytes 2359304 | tf_op jit(solution)/shard_map/ppermute | solution.py:39
  179.9 33.6 %collective-permute-start.38 = (bf16[2,104,3840]{2,1,0:T(8,128)(2,1)}, bf16[2,104,3840]{2,1,0:T(8,128)(2,1)}, u32[]{:S(2)}, u32[]{:S(2)}) collective-permute-start(bf16[2,104,3840]{2,1,0:T(8,128)(2,1)} %add_convert_fusion), channel_id=1, source_target_pairs={{0,16},{4,12},{8,24},{12,4},{16,0},{20,28},{24,8},{28,20},{1,17},{... | collective-permute-start | bytes 4792328 | tf_op jit(solution)/shard_map/ppermute | solution.py:39
  183.4 30.1 %collective-permute-start.37 = (bf16[2,96,3072]{2,1,0:T(8,128)(2,1)}, bf16[2,96,3072]{2,1,0:T(8,128)(2,1)}, u32[]{:S(2)}, u32[]{:S(2)}) collective-permute-start(bf16[2,96,3072]{2,1,0:T(8,128)(2,1)} %add_convert_fusion.1), channel_id=1, source_target_pairs={{0,16},{4,12},{8,24},{12,4},{16,0},{20,28},{24,8},{28,20},{1,17},{... | collective-permute-start | bytes 3538952 | tf_op jit(solution)/shard_map/ppermute | solution.py:39
  218.5 18.8 %collective-permute-start.40 = (bf16[1,104,3840]{2,1,0:T(8,128)(2,1)}, bf16[1,104,3840]{2,1,0:T(8,128)(2,1)}, u32[]{:S(2)}, u32[]{:S(2)}) collective-permute-start(bf16[1,104,3840]{2,1,0:T(8,128)(2,1)} %add_convert_fusion.3), channel_id=1, source_target_pairs={{0,8},{4,20},{8,0},{12,28},{16,24},{20,4},{24,16},{28,12},{1,9},{5... | collective-permute-start | bytes 2396168 | tf_op jit(solution)/shard_map/ppermute | solution.py:39
  218.9 18.3 %collective-permute-start.39 = (bf16[1,96,3072]{2,1,0:T(8,128)(2,1)}, bf16[1,96,3072]{2,1,0:T(8,128)(2,1)}, u32[]{:S(2)}, u32[]{:S(2)}) collective-permute-start(bf16[1,96,3072]{2,1,0:T(8,128)(2,1)} %add_convert_fusion.4), channel_id=1, source_target_pairs={{0,8},{4,20},{8,0},{12,28},{16,24},{20,4},{24,16},{28,12},{1,9},{5... | collective-permute-start | bytes 1769480 | tf_op jit(solution)/shard_map/ppermute | solution.py:39
  222.6 27.0 %collective-permute-start.53 = (bf16[128,768]{1,0:T(8,128)(2,1)}, bf16[128,768]{1,0:T(8,128)(2,1)}, u32[]{:S(2)}, u32[]{:S(2)}) collective-permute-start(bf16[128,768]{1,0:T(8,128)(2,1)} %get-tuple-element.270), channel_id=1, source_target_pairs={{0,2},{1,3},{2,0},{3,1},{4,6},{5,7},{6,4},{7,5},{8,10},{9,11},{10,... | collective-permute-start | bytes 589832 | tf_op jit(solution)/shard_map/ppermute | solution.py:34
  223.1 26.5 %collective-permute-start.52 = (bf16[128,768]{1,0:T(8,128)(2,1)S(1)}, bf16[128,768]{1,0:T(8,128)(2,1)}, u32[]{:S(2)}, u32[]{:S(2)}) collective-permute-start(bf16[128,768]{1,0:T(8,128)(2,1)S(1)} %get-tuple-element.271), channel_id=1, source_target_pairs={{0,1},{1,0},{2,3},{3,2},{4,5},{5,4},{6,7},{7,6},{8,9},{9,8},{10,11... | collective-permute-start | bytes 589832 | tf_op jit(solution)/shard_map/ppermute | solution.py:34
  243.5 23.6 %collective-permute-start.43 = (bf16[2,104,2304]{2,1,0:T(8,128)(2,1)S(1)}, bf16[2,104,2304]{2,1,0:T(8,128)(2,1)S(1)}, u32[]{:S(2)}, u32[]{:S(2)}) collective-permute-start(bf16[2,104,2304]{2,1,0:T(8,128)(2,1)S(1)} %add_convert_fusion.2), channel_id=1, source_target_pairs={{0,16},{4,12},{8,24},{12,4},{16,0},{20,28},{24,8},{28,20},{1,17},{... | collective-permute-start | bytes 2875400 | tf_op jit(solution)/shard_map/ppermute | solution.py:39
  245.2 25.1 %collective-permute-start.48 = (bf16[104,960]{1,0:T(8,128)(2,1)S(1)}, bf16[104,960]{1,0:T(8,128)(2,1)S(1)}, u32[]{:S(2)}, u32[]{:S(2)}) collective-permute-start(bf16[104,960]{1,0:T(8,128)(2,1)S(1)} %pad_maximum_fusion.7), channel_id=1, source_target_pairs={{0,1},{1,0},{2,3},{3,2},{4,5},{5,4},{6,7},{7,6},{8,9},{9,8},{10,11... | collective-permute-start | bytes 599048 | tf_op jit(solution)/shard_map/ppermute | solution.py:34
  260.4 19.9 %collective-permute-start.49 = (bf16[104,960]{1,0:T(8,128)(2,1)S(1)}, bf16[104,960]{1,0:T(8,128)(2,1)S(1)}, u32[]{:S(2)}, u32[]{:S(2)}) collective-permute-start(bf16[104,960]{1,0:T(8,128)(2,1)S(1)} %pad_maximum_fusion.8), channel_id=1, source_target_pairs={{0,2},{1,3},{2,0},{3,1},{4,6},{5,7},{6,4},{7,5},{8,10},{9,11},{10,... | collective-permute-start | bytes 599048 | tf_op jit(solution)/shard_map/ppermute | solution.py:34
  261.6 18.7 %collective-permute-start.50 = (bf16[104,960]{1,0:T(8,128)(2,1)S(1)}, bf16[104,960]{1,0:T(8,128)(2,1)S(1)}, u32[]{:S(2)}, u32[]{:S(2)}) collective-permute-start(bf16[104,960]{1,0:T(8,128)(2,1)S(1)} %pad_maximum_fusion.9), channel_id=1, source_target_pairs={{0,3},{1,2},{2,1},{3,0},{4,7},{5,6},{6,5},{7,4},{8,11},{9,10},{10,... | collective-permute-start | bytes 599048 | tf_op jit(solution)/shard_map/ppermute | solution.py:34
  (67 other events, 666.8 us)

commit v2 on v1

--- a/solution.py
+++ b/solution.py
@@ -64,13 +64,8 @@
     return pieces[:1] + [mp_swap(pieces[step], step) for step in range(1, N_MP)]
 
 
-def from_clips(rows):
-    block = rows.shape[0] // N_MP
-    parts = []
-    for step in range(N_MP):
-        piece = rows[step * block : (step + 1) * block]
-        parts.append(piece if step == 0 else mp_swap(piece, step))
-    return parts
+def from_clips(parts):
+    return parts[:1] + [mp_swap(parts[step], step) for step in range(1, N_MP)]
 
 
 def frames_of(parts, core, depth):
@@ -531,8 +526,8 @@
         cot_far, small_far, refs = refs[:N_MP], refs[N_MP : N_MP + n], refs[N_MP + n :]
         out_p, up_p = refs[:n_out], refs[n_out : n_out + n_up]
         refs = refs[n_out + n_up :]
-        shared_ref, result_out, da_out, do_out = refs[:4]
-        down_outs, mid_outs, refs = refs[4 : 4 + g], refs[4 + g : 4 + 2 * g], refs[4 + 2 * g :]
+        result_outs, shared_ref, da_out, do_out = refs[1 : 1 + N_MP], refs[0], *refs[5:7]
+        down_outs, mid_outs, refs = refs[7 : 7 + g], refs[7 + g : 7 + 2 * g], refs[7 + 2 * g :]
         w_out, sems_out, w_up, sems_up, w_down, sems_down = refs[:6]
         plain, turned, plain_h, turned_h = refs[6:10]
         small_ref, cot_ref, read_sems = refs[10:13]
@@ -581,7 +576,8 @@
         h = n1_ref[...] * row(1) + row(2)
         n2, r2 = norm(h + feed + row(3))
         result_ref[...] = (n2 * row(4) + row(5)).astype(BF16)
-        writes.start(result_ref, result_out)
+        for i, out in enumerate(result_outs):
+            writes.start(result_ref.at[pl.ds(i * block, block)], out)
         for i in range(N_MP):
             cots.get(i)
         gy = cot_ref[...].astype(F32)
@@ -643,7 +639,9 @@
         33,
         [
             like((SHARED, cols), F32),
-            like((rows, width), BF16),
+        ]
+        + [like((rows // N_MP, width), BF16)] * N_MP
+        + [
             like((rows, width), F32),
             like((rows, width), BF16),
         ]
@@ -665,11 +663,11 @@
         + stage_scratch(feed_pieces, cols)
         + [
             pltpu.VMEM((SHARED, cols), BF16),
-            pltpu.SemaphoreType.DMA((3 + n_up,)),
+            pltpu.SemaphoreType.DMA((2 + N_MP + n_up,)),
             pltpu.SemaphoreType.DMA((g * (2 * count + 1),)),
             pltpu.VMEM((1, hidden), F32),
         ],
-        far=3 + 2 * g,
+        far=2 + N_MP + 2 * g,
     )
 
 
@@ -680,7 +678,8 @@
 
     def body(table, da_ref, *refs):
         part_refs, refs = refs[: len(flat)], refs[len(flat) :]
-        pieces, (out_ref, dqkv_ref, held, sems) = refs[:n], refs[n:]
+        pieces, out_refs, refs = refs[:n], refs[n : n + N_MP], refs[n + N_MP :]
+        dqkv_ref, held, sems = refs
         weights = Weights(pieces, table, held, sems, 0, width)
         pair = 0
         for i in range(0, len(flat), 3):
@@ -697,13 +696,15 @@
         value = da_ref[...]
         for i in range(3):
             value = value + dot(dqkv_ref[:, i * width : (i + 1) * width], weights.get(i), NT)
-        out_ref[...] = value.astype(BF16)
+        block = rows // N_MP
+        for i, out_ref in enumerate(out_refs):
+            out_ref[...] = value[i * block : (i + 1) * block].astype(BF16)
 
     return call(
         body,
         "project_back",
         9,
-        [like((rows, width), BF16), like((rows, 3 * width), BF16)],
+        [like((rows // N_MP, width), BF16)] * N_MP + [like((rows, 3 * width), BF16)],
         [da] + flat,
         table,
         pieces,
@@ -882,7 +883,7 @@
     else:
         smalls, small_row = [small.astype(BF16)], 0
     outs = feed(x, mixed, cot_parts, smalls, small_row, table, attn_p, feed_p)
-    mid_shared, result, da, do, *grads = outs
+    mid_shared, result, (da, do), grads = outs[0], list(outs[1:5]), outs[5:7], outs[7:]
     g_down, g_mid = grads[: len(grads) // 2], grads[len(grads) // 2 :]
 
     def by_group_of(value, sizes):
@@ -921,7 +922,7 @@
         other_b, back_a, *result_parts = tie(other_b, back_a, *result_parts)
     back_b = core_swap(other_b)
     parts = [(dq_a, own_a, back_a), (dq_b, own_b, back_b)]
-    frames_grad, dqkv = project_back(da, parts, table, attn_p)
+    *frames_grad, dqkv = project_back(da, parts, table, attn_p)
     grad_parts = from_clips(frames_grad)
     if fast:
         dqkv, b_down, b_mid = tie(dqkv, b_down, b_mid)

time: 304 us -> 298 us (0.980)
  starting transfers between devices: 73.4 us -> 65.4 us
  waiting for transfers between devices: 79.1 us -> 84.4 us
  local copies, waits for them, and re-layouts: 28.2 us -> 24.9 us
    ppermute x27, starting transfers between devices: 55.8 us -> 48.1 us  [mp_swap(): return lax.ppermute(value, 'mp', [(i, i ^ step) for i in range(N_MP)])]
    ppermute x31, waiting for transfers between devices: 26.3 us -> 31.4 us  [dp_swap(): return lax.ppermute(value, 'dp', [(i, target(i)) for i in range(size)])]
    unnamed x73 -> x77, local copies, waits for them, and re-layouts: 13.2 us -> 13.1 us
  transfers between devices with their start and end apart: 58 -> 58, of which waited for: 20 -> 19; matrix products, arithmetic and copies ran while one was open for 12% -> 11% of each run, Pallas kernels for 19% -> 20%
where the time goes in v2:
time: 298 us; the launch traced here: 297 us
  Pallas kernels  92 us (31%)
  waiting for transfers between devices  84.4 us (28%)
  starting transfers between devices  65.4 us (22%)
  other arithmetic  28.2 us (9%)
  local copies, waits for them, and re-layouts  24.9 us (8%)
    pallas_call x4, Pallas kernels, call(): pl.pallas_call(body, out_shape=tuple(outs), in_specs=[pl.BlockSpec(memory...  56.7 us
    ppermute x27, waiting for transfers between devices, mp_swap(): return lax.ppermute(value, 'mp', [(i, i ^ step) for i in range(N_MP)])  53 us
    ppermute x27, starting transfers between devices, mp_swap(): return lax.ppermute(value, 'mp', [(i, i ^ step) for i in range(N_MP)])  48.1 us
    ppermute x31, waiting for transfers between devices, dp_swap(): return lax.ppermute(value, 'dp', [(i, target(i)) for i in range(size)])  31.4 us
    pallas_call x2, Pallas kernels, attend_back(): pl.pallas_call(attend_back_kernel, out_shape=(jax.ShapeDtypeStruct((rows,...  20.8 us
    ppermute x31, starting transfers between devices, dp_swap(): return lax.ppermute(value, 'dp', [(i, target(i)) for i in range(size)])  17.3 us
    pallas_call x1, Pallas kernels, attend(): pl.pallas_call(attend_kernel, out_shape=(jax.ShapeDtypeStruct((rows, widt...  14.6 us
    unnamed x77, local copies, waits for them, and re-layouts  13.1 us
  transfers between devices with their start and end apart: 58, of which 19 were waited for; matrix products, arithmetic and copies ran while one was open for 11% of the time, Pallas kernels for 20%

profile of v2, /device:TPU:0, one launch (start us, length us, event | category | flops | bytes accessed | tf_op | source)
XLA Modules:
  0.0 297.2 jit_solution(6714375651268044685)
XLA Ops:
  4.2 5.1 %collective-permute-start.2 = (bf16[104,768]{1,0:T(8,128)(2,1)S(1)}, bf16[104,768]{1,0:T(8,128)(2,1)S(1)}, u32[]{:S(2)}, u32[]{:S(2)}) collective-permute-start(bf16[104,768]{1,0:T(8,128)(2,1)S(1)} %pad_maximum_fusion.10), channel_id=1, source_target_pairs={{0,3},{1,2},{2,1},{3,0},{4,7},{5,6},{6,5},{7,4},{8,11},{9,10},{10,... | collective-permute-start | bytes 479240 | tf_op jit(solution)/shard_map/ppermute | solution.py:34
  19.6 3.4 %collective-permute-done.1 = bf16[104,768]{1,0:T(8,128)(2,1)S(1)} collective-permute-done((bf16[104,768]{1,0:T(8,128)(2,1)S(1)}, bf16[104,768]{1,0:T(8,128)(2,1)S(1)}, u32[]{:S(2)}, u32[]{:S(2)}) %collective-permute-start.1) | collective-permute-done | bytes 159776 | tf_op jit(solution)/shard_map/ppermute | solution.py:34
  31.4 9.1 %collective-permute-done.15 = bf16[104,1536]{1,0:T(8,128)(2,1)S(1)} collective-permute-done((bf16[104,1536]{1,0:T(8,128)(2,1)S(1)}, bf16[104,1536]{1,0:T(8,128)(2,1)S(1)}, u32[]{:S(2)}, u32[]{:S(2)}) %collective-permute-start.15) | collective-permute-done | bytes 319520 | tf_op jit(solution)/shard_map/ppermute | solution.py:34
  40.5 11.5 %collective-permute-start.13 = (bf16[104,1536]{1,0:T(8,128)(2,1)S(1)}, bf16[104,1536]{1,0:T(8,128)(2,1)S(1)}, u32[]{:S(2)}, u32[]{:S(2)}) collective-permute-start(bf16[104,1536]{1,0:T(8,128)(2,1)S(1)} %pad_maximum_fusion.5), channel_id=1, source_target_pairs={{0,1},{1,0},{2,3},{3,2},{4,5},{5,4},{6,7},{7,6},{8,9},{9,8},{10,11... | collective-permute-start | bytes 958472 | tf_op jit(solution)/shard_map/ppermute | solution.py:34
  52.0 3.7 %collective-permute-done.14 = bf16[104,1536]{1,0:T(8,128)(2,1)S(1)} collective-permute-done((bf16[104,1536]{1,0:T(8,128)(2,1)S(1)}, bf16[104,1536]{1,0:T(8,128)(2,1)S(1)}, u32[]{:S(2)}, u32[]{:S(2)}) %collective-permute-start.14) | collective-permute-done | bytes 319520 | tf_op jit(solution)/shard_map/ppermute | solution.py:34
  56.8 3.7 %collective-permute-done.13 = bf16[104,1536]{1,0:T(8,128)(2,1)S(1)} collective-permute-done((bf16[104,1536]{1,0:T(8,128)(2,1)S(1)}, bf16[104,1536]{1,0:T(8,128)(2,1)S(1)}, u32[]{:S(2)}, u32[]{:S(2)}) %collective-permute-start.13) | collective-permute-done | bytes 319520 | tf_op jit(solution)/shard_map/ppermute | solution.py:34
  60.7 3.3 %collective-permute-start.17 = (bf16[128,768]{1,0:T(8,128)(2,1)S(1)}, bf16[128,768]{1,0:T(8,128)(2,1)S(1)}, u32[]{:S(2)}, u32[]{:S(2)}) collective-permute-start(bf16[128,768]{1,0:T(8,128)(2,1)S(1)} %get-tuple-element.137), channel_id=1, source_target_pairs={{0,2},{1,3},{2,0},{3,1},{4,6},{5,7},{6,4},{7,5},{8,10},{9,11},{10,... | collective-permute-start | bytes 589832 | tf_op jit(solution)/shard_map/ppermute | solution.py:34
  73.5 4.8 %collective-permute-done.17.refs_2_ = bf16[128,768]{1,0:T(8,128)(2,1)S(1)} collective-permute-done((bf16[128,768]{1,0:T(8,128)(2,1)S(1)}, bf16[128,768]{1,0:T(8,128)(2,1)S(1)}, u32[]{:S(2)}, u32[]{:S(2)}) %collective-permute-start.17) | collective-permute-done | bytes 196640 | tf_op jit(solution)/shard_map/ppermute | solution.py:34
  83.3 7.4 %project.1 = (bf16[512,768]{1,0:T(8,128)(2,1)}, bf16[512,2304]{1,0:T(8,128)(2,1)}, bf16[512,1536]{1,0:T(8,128)(2,1)}) custom-call(s32[8]{0:T(128)} %stack.122.table, bf16[128,768]{1,0:T(8,128)(2,1)} %get-tuple-element.148.refs_0_, bf16[128,768]{1,0:T(8,128)(2,1)} %copy-done.26, bf16[128,768]{1,0:T(8,128)(2,1)} %copy-done.27, bf16[128,768]{1,0:T(8,128)(2,1)} %copy-done.28, ...), custom_call_target="tpu_custom_call" | custom-call | flops 2310000128 | bytes 210000 | tf_op jit(solution)/shard_map/project/pallas_call | solution.py:296
  90.8 10.5 %collective-permute-done.20.refs_6_.refs_22_ = bf16[104,6144]{1,0:T(8,128)(2,1)} collective-permute-done((bf16[104,6144]{1,0:T(8,128)(2,1)}, bf16[104,6144]{1,0:T(8,128)(2,1)}, u32[]{:S(2)}, u32[]{:S(2)}) %collective-permute-start.20) | collective-permute-done | bytes 1277984 | tf_op jit(solution)/shard_map/ppermute | solution.py:39
  106.3 14.6 %attend.1 = (bf16[512,768]{1,0:T(8,128)(2,1)}, f32[512,768]{1,0:T(8,128)}) custom-call(bf16[512,2304]{1,0:T(8,128)(2,1)} %get-tuple-element.161.q_ref.k_ref.v_ref, bf16[512,2304]{1,0:T(8,128)(2,1)} %get-tuple-element.161.q_ref.k_ref.v_ref, bf16[512,2304]{1,0:T(8,128)(2,1)} %get-tuple-element.161.q_ref.k_ref.v_ref, bf16[512,1536]{1,0:T(8,128)(2,1)} %copy-done, ...), custom_call_target="tpu_custom_call" | custom-call | flops 4950000128 | bytes 450000 | tf_op jit(solution)/shard_map/attend/pallas_call | solution.py:342
  122.2 3.0 %collective-permute-done.29.refs_11_.refs_27_ = bf16[104,6144]{1,0:T(8,128)(2,1)S(1)} collective-permute-done((bf16[104,6144]{1,0:T(8,128)(2,1)S(1)}, bf16[104,6144]{1,0:T(8,128)(2,1)S(1)}, u32[]{:S(2)}, u32[]{:S(2)}) %collective-permute-start.29) | collective-permute-done | bytes 1277984 | tf_op jit(solution)/shard_map/ppermute | solution.py:39
  126.2 33.0 %feed.1 = (f32[8,3840]{1,0:T(8,128)}, bf16[128,768]{1,0:T(8,128)(2,1)}, bf16[128,768]{1,0:T(8,128)(2,1)}, bf16[128,768]{1,0:T(8,128)(2,1)}, bf16[128,768]{1,0:T(...) custom-call(s32[8]{0:T(128)} %stack.122.table, ...), custom_call_target="tpu_custom_call" | custom-call | flops 10890000384 | bytes 990000 | tf_op jit(solution)/shard_map/feed/pallas_call | solution.py:296
  162.0 10.4 %attend_back.2 = (bf16[512,384]{1,0:T(8,128)(2,1)}, f32[512,768]{1,0:T(8,128)}, bf16[512,768]{1,0:T(8,128)(2,1)}) custom-call(bf16[512,2304]{1,0:T(8,128)(2,1)} %get-tuple-element.161.q_ref.k_ref.v_ref, bf16[512,2304]{1,0:T(8,128)(2,1)} %get-tuple-element.161.q_ref.k_ref.v_ref, bf16[512,2304]{1,0:T(8,128)(2,1)} %get-tuple-element.161.q_ref.k_ref.v_ref, ...), custom_call_target="tpu_custom_call" | custom-call | flops 2969999872 | bytes 270000 | tf_op jit(solution)/shard_map/attend_back/pallas_call | solution.py:405
  182.8 10.4 %attend_back.3 = (bf16[512,384]{1,0:T(8,128)(2,1)}, f32[512,768]{1,0:T(8,128)}, bf16[512,768]{1,0:T(8,128)(2,1)}) custom-call(bf16[512,2304]{1,0:T(8,128)(2,1)} %get-tuple-element.161.q_ref.k_ref.v_ref, bf16[512,2304]{1,0:T(8,128)(2,1)} %get-tuple-element.161.q_ref.k_ref.v_ref, bf16[512,2304]{1,0:T(8,128)(2,1)} %get-tuple-element.161.q_ref.k_ref.v_ref, ...), custom_call_target="tpu_custom_call" | custom-call | flops 2969999872 | bytes 270000 | tf_op jit(solution)/shard_map/attend_back/pallas_call | solution.py:405
  196.0 9.4 %project_back.1 = (bf16[128,768]{1,0:T(8,128)(2,1)}, bf16[128,768]{1,0:T(8,128)(2,1)}, bf16[128,768]{1,0:T(8,128)(2,1)}, bf16[128,768]{1,0:T(8,128)(2,1)}, bf16[512,2304]{1,0:T(8,128)(2,1)}) custom-call(s32[8]{0:T(128)} %stack.122.table, f32[512,768]{1,0:T(8,128)} %get-tuple-element.181.da_ref, bf16[512,384]{1,0:T(8,128)(2,1)} %get-tuple-element.184.refs_0_, ...), custom_call_target="tpu_custom_call" | custom-call | flops 2969999872 | bytes 270000 | tf_op jit(solution)/shard_map/project_back/pallas_call | solution.py:296
  205.4 6.8 %collective-permute-done.37 = bf16[2,96,3072]{2,1,0:T(8,128)(2,1)} collective-permute-done((bf16[2,96,3072]{2,1,0:T(8,128)(2,1)}, bf16[2,96,3072]{2,1,0:T(8,128)(2,1)}, u32[]{:S(2)}, u32[]{:S(2)}) %collective-permute-start.37) | collective-permute-done | bytes 1179680 | tf_op jit(solution)/shard_map/ppermute | solution.py:39
  223.6 6.8 %project_grads.1 = (f32[8,2304]{1,0:T(8,128)}, bf16[4,104,2304]{2,1,0:T(8,128)(2,1)}, bf16[4,104,2304]{2,1,0:T(8,128)(2,1)}) custom-call(s32[8]{0:T(128)} %stack.122.table, bf16[512,768]{1,0:T(8,128)(2,1)} %get-tuple-element.160.x_ref, bf16[512,2304]{1,0:T(8,128)(2,1)} %get-tuple-element.212.dqkv_ref), custom_call_target="tpu_custom_call" | custom-call | flops 2310000128 | bytes 210000 | tf_op jit(solution)/shard_map/project_grads/pallas_call | solution.py:296
  230.4 5.5 %collective-permute-done.39 = bf16[1,96,3072]{2,1,0:T(8,128)(2,1)} collective-permute-done((bf16[1,96,3072]{2,1,0:T(8,128)(2,1)}, bf16[1,96,3072]{2,1,0:T(8,128)(2,1)}, u32[]{:S(2)}, u32[]{:S(2)}) %collective-permute-start.39) | collective-permute-done | bytes 589856 | tf_op jit(solution)/shard_map/ppermute | solution.py:39
  250.6 6.5 %collective-permute-done.44 = bf16[96,768]{1,0:T(8,128)(2,1)S(1)} collective-permute-done((bf16[96,768]{1,0:T(8,128)(2,1)S(1)}, bf16[96,768]{1,0:T(8,128)(2,1)S(1)}, u32[]{:S(2)}, u32[]{:S(2)}) %collective-permute-start.44) | collective-permute-done | bytes 147488 | tf_op jit(solution)/shard_map/ppermute | solution.py:34
  257.0 10.6 %collective-permute-done.45 = bf16[96,768]{1,0:T(8,128)(2,1)S(1)} collective-permute-done((bf16[96,768]{1,0:T(8,128)(2,1)S(1)}, bf16[96,768]{1,0:T(8,128)(2,1)S(1)}, u32[]{:S(2)}, u32[]{:S(2)}) %collective-permute-start.45) | collective-permute-done | bytes 147488 | tf_op jit(solution)/shard_map/ppermute | solution.py:34
  272.3 5.4 %collective-permute-done.49 = bf16[104,960]{1,0:T(8,128)(2,1)S(1)} collective-permute-done((bf16[104,960]{1,0:T(8,128)(2,1)S(1)}, bf16[104,960]{1,0:T(8,128)(2,1)S(1)}, u32[]{:S(2)}, u32[]{:S(2)}) %collective-permute-start.49) | collective-permute-done | bytes 199712 | tf_op jit(solution)/shard_map/ppermute | solution.py:34
  281.4 3.0 %collective-permute-start.56 = (bf16[104,576]{1,0:T(8,128)(2,1)S(1)}, bf16[104,576]{1,0:T(8,128)(2,1)S(1)}, u32[]{:S(2)}, u32[]{:S(2)}) collective-permute-start(bf16[104,576]{1,0:T(8,128)(2,1)S(1)} %pad_maximum_fusion.12), channel_id=1, source_target_pairs={{0,2},{1,3},{2,0},{3,1},{4,6},{5,7},{6,4},{7,5},{8,10},{9,11},{10,... | collective-permute-start | bytes 359432 | tf_op jit(solution)/shard_map/ppermute | solution.py:34
  288.9 5.6 %collective-permute-done.56 = bf16[104,576]{1,0:T(8,128)(2,1)S(1)} collective-permute-done((bf16[104,576]{1,0:T(8,128)(2,1)S(1)}, bf16[104,576]{1,0:T(8,128)(2,1)S(1)}, u32[]{:S(2)}, u32[]{:S(2)}) %collective-permute-start.56) | collective-permute-done | bytes 119840 | tf_op jit(solution)/shard_map/ppermute | solution.py:34
  (268 shorter events, 101.3 us)
Async XLA Ops:
  24.0 31.7 %collective-permute-start.8 = (bf16[104,3072]{1,0:T(8,128)(2,1)S(1)}, bf16[104,3072]{1,0:T(8,128)(2,1)}, u32[]{:S(2)}, u32[]{:S(2)}) collective-permute-start(bf16[104,3072]{1,0:T(8,128)(2,1)S(1)} %maximum_maximum_fusion.refs_5_.refs_12_.refs_6_), channel_id=1, source_target_pairs={{0,24},{4,28},{8,16},{12,20},{16,8},{20,12},{24,0},{28,4},{1,25},{... | collective-permute-start | bytes 1916936 | tf_op jit(solution)/shard_map/ppermute | solution.py:39
  26.5 29.7 %collective-permute-start.7 = (bf16[104,3072]{1,0:T(8,128)(2,1)S(1)}, bf16[104,3072]{1,0:T(8,128)(2,1)}, u32[]{:S(2)}, u32[]{:S(2)}) collective-permute-start(bf16[104,3072]{1,0:T(8,128)(2,1)S(1)} %maximum_maximum_fusion.refs_5_.refs_12_.refs_6_), channel_id=1, source_target_pairs={{0,16},{4,12},{8,24},{12,4},{16,0},{20,28},{24,8},{28,20},{1,17},{... | collective-permute-start | bytes 1916936 | tf_op jit(solution)/shard_map/ppermute | solution.py:39
  27.0 29.3 %collective-permute-start.6 = (bf16[104,3072]{1,0:T(8,128)(2,1)S(1)}, bf16[104,3072]{1,0:T(8,128)(2,1)}, u32[]{:S(2)}, u32[]{:S(2)}) collective-permute-start(bf16[104,3072]{1,0:T(8,128)(2,1)S(1)} %maximum_maximum_fusion.refs_5_.refs_12_.refs_6_), channel_id=1, source_target_pairs={{0,8},{4,20},{8,0},{12,28},{16,24},{20,4},{24,16},{28,12},{1,9},{5... | collective-permute-start | bytes 1916936 | tf_op jit(solution)/shard_map/ppermute | solution.py:39
  30.7 25.0 %collective-permute-start.14 = (bf16[104,1536]{1,0:T(8,128)(2,1)S(1)}, bf16[104,1536]{1,0:T(8,128)(2,1)S(1)}, u32[]{:S(2)}, u32[]{:S(2)}) collective-permute-start(bf16[104,1536]{1,0:T(8,128)(2,1)S(1)} %pad_maximum_fusion.5), channel_id=1, source_target_pairs={{0,2},{1,3},{2,0},{3,1},{4,6},{5,7},{6,4},{7,5},{8,10},{9,11},{10,... | collective-permute-start | bytes 958472 | tf_op jit(solution)/shard_map/ppermute | solution.py:34
  40.5 20.0 %collective-permute-start.13 = (bf16[104,1536]{1,0:T(8,128)(2,1)S(1)}, bf16[104,1536]{1,0:T(8,128)(2,1)S(1)}, u32[]{:S(2)}, u32[]{:S(2)}) collective-permute-start(bf16[104,1536]{1,0:T(8,128)(2,1)S(1)} %pad_maximum_fusion.5), channel_id=1, source_target_pairs={{0,1},{1,0},{2,3},{3,2},{4,5},{5,4},{6,7},{7,6},{8,9},{9,8},{10,11... | collective-permute-start | bytes 958472 | tf_op jit(solution)/shard_map/ppermute | solution.py:34
  70.7 30.6 %collective-permute-start.20 = (bf16[104,6144]{1,0:T(8,128)(2,1)}, bf16[104,6144]{1,0:T(8,128)(2,1)}, u32[]{:S(2)}, u32[]{:S(2)}) collective-permute-start(bf16[104,6144]{1,0:T(8,128)(2,1)} %constant_dynamic-update-slice_fusion.refs_4_.refs_20_), channel_id=1, source_target_pairs={{0,16},{4,12},{8,24},{12,4},{16,0},{20,28},{24,8},{28,20},{1,17},{... | collective-permute-start | bytes 3833864 | tf_op jit(solution)/shard_map/ppermute | solution.py:39
  72.0 29.3 %collective-permute-start.19 = (bf16[104,6144]{1,0:T(8,128)(2,1)}, bf16[104,6144]{1,0:T(8,128)(2,1)}, u32[]{:S(2)}, u32[]{:S(2)}) collective-permute-start(bf16[104,6144]{1,0:T(8,128)(2,1)} %constant_dynamic-update-slice_fusion.refs_4_.refs_20_), channel_id=1, source_target_pairs={{0,8},{4,20},{8,0},{12,28},{16,24},{20,4},{24,16},{28,12},{1,9},{5... | collective-permute-start | bytes 3833864 | tf_op jit(solution)/shard_map/ppermute | solution.py:39
  78.3 23.0 %collective-permute-start.22 = (bf16[104,6144]{1,0:T(8,128)(2,1)}, bf16[104,6144]{1,0:T(8,128)(2,1)}, u32[]{:S(2)}, u32[]{:S(2)}) collective-permute-start(bf16[104,6144]{1,0:T(8,128)(2,1)} %constant_dynamic-update-slice_fusion.refs_4_.refs_20_), channel_id=1, source_target_pairs={{0,4},{4,0},{8,12},{12,8},{16,20},{20,16},{24,28},{28,24},{1,5},{5... | collective-permute-start | bytes 3833864 | tf_op jit(solution)/shard_map/ppermute | solution.py:39
  101.3 19.7 %collective-permute-start.26 = (bf16[104,6144]{1,0:T(8,128)(2,1)}, bf16[104,6144]{1,0:T(8,128)(2,1)S(1)}, u32[]{:S(2)}, u32[]{:S(2)}) collective-permute-start(bf16[104,6144]{1,0:T(8,128)(2,1)} %collective-permute-done.20.refs_6_.refs_22_), channel_id=1, source_target_pairs={{0,4},{4,0},{8,12},{12,8},{16,20},{20,16},{24,28},{28,24},{1,5},{5... | collective-permute-start | bytes 3833864 | tf_op jit(solution)/shard_map/ppermute | solution.py:39
  101.8 19.2 %collective-permute-start.25 = (bf16[104,6144]{1,0:T(8,128)(2,1)}, bf16[104,6144]{1,0:T(8,128)(2,1)S(1)}, u32[]{:S(2)}, u32[]{:S(2)}) collective-permute-start(bf16[104,6144]{1,0:T(8,128)(2,1)} %collective-permute-done.19.refs_5_.refs_21_), channel_id=1, source_target_pairs={{0,4},{4,0},{8,12},{12,8},{16,20},{20,16},{24,28},{28,24},{1,5},{5... | collective-permute-start | bytes 3833864 | tf_op jit(solution)/shard_map/ppermute | solution.py:39
  101.9 19.2 %collective-permute-start.24 = (bf16[104,6144]{1,0:T(8,128)(2,1)}, bf16[104,6144]{1,0:T(8,128)(2,1)S(1)}, u32[]{:S(2)}, u32[]{:S(2)}) collective-permute-start(bf16[104,6144]{1,0:T(8,128)(2,1)} %collective-permute-done.19.refs_5_.refs_21_), channel_id=1, source_target_pairs={{0,16},{4,12},{8,24},{12,4},{16,0},{20,28},{24,8},{28,20},{1,17},{... | collective-permute-start | bytes 3833864 | tf_op jit(solution)/shard_map/ppermute | solution.py:39
  103.4 17.6 %collective-permute-start.28 = (bf16[128,768]{1,0:T(8,128)(2,1)S(1)}, bf16[128,768]{1,0:T(8,128)(2,1)S(1)}, u32[]{:S(2)}, u32[]{:S(2)}) collective-permute-start(bf16[128,768]{1,0:T(8,128)(2,1)S(1)} %get-tuple-element.284), channel_id=1, source_target_pairs={{0,2},{1,3},{2,0},{3,1},{4,6},{5,7},{6,4},{7,5},{8,10},{9,11},{10,... | collective-permute-start | bytes 589832 | tf_op jit(solution)/shard_map/ppermute | solution.py:34
  172.4 20.9 %collective-permute-start.33 = (bf16[512,768]{1,0:T(8,128)(2,1)}, bf16[512,768]{1,0:T(8,128)(2,1)}, u32[]{:S(2)}, u32[]{:S(2)}) collective-permute-start(bf16[512,768]{1,0:T(8,128)(2,1)} %get-tuple-element.197), channel_id=1, source_target_pairs={{0,4},{4,0},{8,12},{12,8},{16,20},{20,16},{24,28},{28,24},{1,5},{5... | collective-permute-start | bytes 2359304 | tf_op jit(solution)/shard_map/ppermute | solution.py:39
  178.5 33.6 %collective-permute-start.38 = (bf16[2,104,3840]{2,1,0:T(8,128)(2,1)}, bf16[2,104,3840]{2,1,0:T(8,128)(2,1)}, u32[]{:S(2)}, u32[]{:S(2)}) collective-permute-start(bf16[2,104,3840]{2,1,0:T(8,128)(2,1)} %add_convert_fusion), channel_id=1, source_target_pairs={{0,16},{4,12},{8,24},{12,4},{16,0},{20,28},{24,8},{28,20},{1,17},{... | collective-permute-start | bytes 4792328 | tf_op jit(solution)/shard_map/ppermute | solution.py:39
  182.1 30.1 %collective-permute-start.37 = (bf16[2,96,3072]{2,1,0:T(8,128)(2,1)}, bf16[2,96,3072]{2,1,0:T(8,128)(2,1)}, u32[]{:S(2)}, u32[]{:S(2)}) collective-permute-start(bf16[2,96,3072]{2,1,0:T(8,128)(2,1)} %add_convert_fusion.1), channel_id=1, source_target_pairs={{0,16},{4,12},{8,24},{12,4},{16,0},{20,28},{24,8},{28,20},{1,17},{... | collective-permute-start | bytes 3538952 | tf_op jit(solution)/shard_map/ppermute | solution.py:39
  217.2 18.8 %collective-permute-start.40 = (bf16[1,104,3840]{2,1,0:T(8,128)(2,1)}, bf16[1,104,3840]{2,1,0:T(8,128)(2,1)}, u32[]{:S(2)}, u32[]{:S(2)}) collective-permute-start(bf16[1,104,3840]{2,1,0:T(8,128)(2,1)} %add_convert_fusion.3), channel_id=1, source_target_pairs={{0,8},{4,20},{8,0},{12,28},{16,24},{20,4},{24,16},{28,12},{1,9},{5... | collective-permute-start | bytes 2396168 | tf_op jit(solution)/shard_map/ppermute | solution.py:39
  217.6 18.4 %collective-permute-start.39 = (bf16[1,96,3072]{2,1,0:T(8,128)(2,1)}, bf16[1,96,3072]{2,1,0:T(8,128)(2,1)}, u32[]{:S(2)}, u32[]{:S(2)}) collective-permute-start(bf16[1,96,3072]{2,1,0:T(8,128)(2,1)} %add_convert_fusion.4), channel_id=1, source_target_pairs={{0,8},{4,20},{8,0},{12,28},{16,24},{20,4},{24,16},{28,12},{1,9},{5... | collective-permute-start | bytes 1769480 | tf_op jit(solution)/shard_map/ppermute | solution.py:39
  220.9 23.0 %collective-permute-start.52 = (bf16[128,768]{1,0:T(8,128)(2,1)}, bf16[128,768]{1,0:T(8,128)(2,1)S(1)}, u32[]{:S(2)}, u32[]{:S(2)}) collective-permute-start(bf16[128,768]{1,0:T(8,128)(2,1)} %get-tuple-element.236), channel_id=1, source_target_pairs={{0,1},{1,0},{2,3},{3,2},{4,5},{5,4},{6,7},{7,6},{8,9},{9,8},{10,11... | collective-permute-start | bytes 589832 | tf_op jit(solution)/shard_map/ppermute | solution.py:34
  220.9 23.1 %collective-permute-start.53 = (bf16[128,768]{1,0:T(8,128)(2,1)}, bf16[128,768]{1,0:T(8,128)(2,1)}, u32[]{:S(2)}, u32[]{:S(2)}) collective-permute-start(bf16[128,768]{1,0:T(8,128)(2,1)} %get-tuple-element.237), channel_id=1, source_target_pairs={{0,2},{1,3},{2,0},{3,1},{4,6},{5,7},{6,4},{7,5},{8,10},{9,11},{10,... | collective-permute-start | bytes 589832 | tf_op jit(solution)/shard_map/ppermute | solution.py:34
  242.1 26.9 %collective-permute-start.43 = (bf16[2,104,2304]{2,1,0:T(8,128)(2,1)S(1)}, bf16[2,104,2304]{2,1,0:T(8,128)(2,1)S(1)}, u32[]{:S(2)}, u32[]{:S(2)}) collective-permute-start(bf16[2,104,2304]{2,1,0:T(8,128)(2,1)S(1)} %add_convert_fusion.2), channel_id=1, source_target_pairs={{0,16},{4,12},{8,24},{12,4},{16,0},{20,28},{24,8},{28,20},{1,17},{... | collective-permute-start | bytes 2875400 | tf_op jit(solution)/shard_map/ppermute | solution.py:39
  243.8 28.4 %collective-permute-start.48 = (bf16[104,960]{1,0:T(8,128)(2,1)S(1)}, bf16[104,960]{1,0:T(8,128)(2,1)S(1)}, u32[]{:S(2)}, u32[]{:S(2)}) collective-permute-start(bf16[104,960]{1,0:T(8,128)(2,1)S(1)} %pad_maximum_fusion.7), channel_id=1, source_target_pairs={{0,1},{1,0},{2,3},{3,2},{4,5},{5,4},{6,7},{7,6},{8,9},{9,8},{10,11... | collective-permute-start | bytes 599048 | tf_op jit(solution)/shard_map/ppermute | solution.py:34
  247.2 20.5 %collective-permute-start.45 = (bf16[96,768]{1,0:T(8,128)(2,1)S(1)}, bf16[96,768]{1,0:T(8,128)(2,1)S(1)}, u32[]{:S(2)}, u32[]{:S(2)}) collective-permute-start(bf16[96,768]{1,0:T(8,128)(2,1)S(1)} %get-tuple-element.223), channel_id=1, source_target_pairs={{0,2},{1,3},{2,0},{3,1},{4,6},{5,7},{6,4},{7,5},{8,10},{9,11},{10,... | collective-permute-start | bytes 442376 | tf_op jit(solution)/shard_map/ppermute | solution.py:34
  247.5 21.5 %collective-permute-start.46 = (bf16[96,768]{1,0:T(8,128)(2,1)S(1)}, bf16[96,768]{1,0:T(8,128)(2,1)S(1)}, u32[]{:S(2)}, u32[]{:S(2)}) collective-permute-start(bf16[96,768]{1,0:T(8,128)(2,1)S(1)} %get-tuple-element.224), channel_id=1, source_target_pairs={{0,3},{1,2},{2,1},{3,0},{4,7},{5,6},{6,5},{7,4},{8,11},{9,10},{10,... | collective-permute-start | bytes 442376 | tf_op jit(solution)/shard_map/ppermute | solution.py:34
  257.0 20.6 %collective-permute-start.49 = (bf16[104,960]{1,0:T(8,128)(2,1)S(1)}, bf16[104,960]{1,0:T(8,128)(2,1)S(1)}, u32[]{:S(2)}, u32[]{:S(2)}) collective-permute-start(bf16[104,960]{1,0:T(8,128)(2,1)S(1)} %pad_maximum_fusion.8), channel_id=1, source_target_pairs={{0,2},{1,3},{2,0},{3,1},{4,6},{5,7},{6,4},{7,5},{8,10},{9,11},{10,... | collective-permute-start | bytes 599048 | tf_op jit(solution)/shard_map/ppermute | solution.py:34
  (69 other events, 668.7 us)

commit v3 on v2

--- a/solution.py
+++ b/solution.py
@@ -933,13 +933,13 @@
         b_mid = dp_swap(a_mid, early)
     attn_shared, *g_attn = project_grads(x, dqkv, table, attn_p)
     if fast:
-        both = tie(*g_attn, b_down, b_mid, grad_parts[3])
-        g_attn, b_down, b_mid, grad_parts[3] = both[:2], both[2], both[3], both[4]
+        both = tie(*g_attn, b_down, b_mid, *grad_parts)
+        g_attn, b_down, b_mid, grad_parts = both[:2], both[2], both[3], both[4:]
         b_attn = core_swap(g_attn[1])
         s_down = by_group_of(last_sum(stays(t_down, b_down)), [units])
         t_attn = [g_attn[0], b_attn]
         a_attn = goes_on(t_attn)
-        a_attn, *s_down = tie(a_attn, *s_down)
+        a_attn, b_mid, *s_down = tie(a_attn, b_mid, *s_down)
         b_attn = dp_swap(a_attn, late)
         z_down = mp_away(s_down)
         s_mid = by_group_of(last_sum(stays(t_mid, b_mid)), [units, group])

time: 298 us -> 306 us (1.027)
  starting transfers between devices: 65.4 us -> 72.8 us
  other arithmetic: 28.2 us -> 32.3 us
    ppermute x31, waiting for transfers between devices: 31.4 us -> 24.7 us  [dp_swap(): return lax.ppermute(value, 'dp', [(i, target(i)) for i in range(size)])]
    ppermute x27, starting transfers between devices: 48.1 us -> 53.4 us  [mp_swap(): return lax.ppermute(value, 'mp', [(i, i ^ step) for i in range(N_MP)])]
    ppermute x27, waiting for transfers between devices: 53 us -> 56.8 us  [mp_swap(): return lax.ppermute(value, 'mp', [(i, i ^ step) for i in range(N_MP)])]
    unnamed x77 -> x81, local copies, waits for them, and re-layouts: 13.1 us -> 12 us
  transfers between devices with their start and end apart: 58 -> 58, of which waited for: 19 -> 19; matrix products, arithmetic and copies ran while one was open for 11% -> 11% of each run, Pallas kernels for 20% -> 19%
where the time goes in v3:
time: 306 us; the launch traced here: 304 us
  Pallas kernels  92.1 us (30%)
  waiting for transfers between devices  81.4 us (27%)
  starting transfers between devices  72.8 us (24%)
  other arithmetic  32.3 us (11%)
  local copies, waits for them, and re-layouts  23.6 us (8%)
    ppermute x27, waiting for transfers between devices, mp_swap(): return lax.ppermute(value, 'mp', [(i, i ^ step) for i in range(N_MP)])  56.8 us
    pallas_call x4, Pallas kernels, call(): pl.pallas_call(body, out_shape=tuple(outs), in_specs=[pl.BlockSpec(memory...  56.7 us
    ppermute x27, starting transfers between devices, mp_swap(): return lax.ppermute(value, 'mp', [(i, i ^ step) for i in range(N_MP)])  53.4 us
    ppermute x31, waiting for transfers between devices, dp_swap(): return lax.ppermute(value, 'dp', [(i, target(i)) for i in range(size)])  24.7 us
    pallas_call x2, Pallas kernels, attend_back(): pl.pallas_call(attend_back_kernel, out_shape=(jax.ShapeDtypeStruct((rows,...  20.8 us
    ppermute x31, starting transfers between devices, dp_swap(): return lax.ppermute(value, 'dp', [(i, target(i)) for i in range(size)])  19.4 us
    pallas_call x1, Pallas kernels, attend(): pl.pallas_call(attend_kernel, out_shape=(jax.ShapeDtypeStruct((rows, widt...  14.6 us
    convert_element_type x6, other arithmetic, goes_on(): return sum((term[half:].astype(F32) for term in terms)).astype(BF16)  12.1 us
  transfers between devices with their start and end apart: 58, of which 19 were waited for; matrix products, arithmetic and copies ran while one was open for 11% of the time, Pallas kernels for 19%

profile of v3, /device:TPU:0, one launch (start us, length us, event | category | flops | bytes accessed | tf_op | source)
XLA Modules:
  0.0 304.5 jit_solution(17938943466914583948)
XLA Ops:
  4.2 5.1 %collective-permute-start.2 = (bf16[104,768]{1,0:T(8,128)(2,1)S(1)}, bf16[104,768]{1,0:T(8,128)(2,1)S(1)}, u32[]{:S(2)}, u32[]{:S(2)}) collective-permute-start(bf16[104,768]{1,0:T(8,128)(2,1)S(1)} %pad_maximum_fusion.10), channel_id=1, source_target_pairs={{0,3},{1,2},{2,1},{3,0},{4,7},{5,6},{6,5},{7,4},{8,11},{9,10},{10,... | collective-permute-start | bytes 479240 | tf_op jit(solution)/shard_map/ppermute | solution.py:34
  19.6 3.4 %collective-permute-done.1 = bf16[104,768]{1,0:T(8,128)(2,1)S(1)} collective-permute-done((bf16[104,768]{1,0:T(8,128)(2,1)S(1)}, bf16[104,768]{1,0:T(8,128)(2,1)S(1)}, u32[]{:S(2)}, u32[]{:S(2)}) %collective-permute-start.1) | collective-permute-done | bytes 159776 | tf_op jit(solution)/shard_map/ppermute | solution.py:34
  31.4 9.1 %collective-permute-done.15 = bf16[104,1536]{1,0:T(8,128)(2,1)S(1)} collective-permute-done((bf16[104,1536]{1,0:T(8,128)(2,1)S(1)}, bf16[104,1536]{1,0:T(8,128)(2,1)S(1)}, u32[]{:S(2)}, u32[]{:S(2)}) %collective-permute-start.15) | collective-permute-done | bytes 319520 | tf_op jit(solution)/shard_map/ppermute | solution.py:34
  40.5 11.5 %collective-permute-start.13 = (bf16[104,1536]{1,0:T(8,128)(2,1)S(1)}, bf16[104,1536]{1,0:T(8,128)(2,1)S(1)}, u32[]{:S(2)}, u32[]{:S(2)}) collective-permute-start(bf16[104,1536]{1,0:T(8,128)(2,1)S(1)} %pad_maximum_fusion.5), channel_id=1, source_target_pairs={{0,1},{1,0},{2,3},{3,2},{4,5},{5,4},{6,7},{7,6},{8,9},{9,8},{10,11... | collective-permute-start | bytes 958472 | tf_op jit(solution)/shard_map/ppermute | solution.py:34
  52.0 3.7 %collective-permute-done.14 = bf16[104,1536]{1,0:T(8,128)(2,1)S(1)} collective-permute-done((bf16[104,1536]{1,0:T(8,128)(2,1)S(1)}, bf16[104,1536]{1,0:T(8,128)(2,1)S(1)}, u32[]{:S(2)}, u32[]{:S(2)}) %collective-permute-start.14) | collective-permute-done | bytes 319520 | tf_op jit(solution)/shard_map/ppermute | solution.py:34
  56.7 3.7 %collective-permute-done.13 = bf16[104,1536]{1,0:T(8,128)(2,1)S(1)} collective-permute-done((bf16[104,1536]{1,0:T(8,128)(2,1)S(1)}, bf16[104,1536]{1,0:T(8,128)(2,1)S(1)}, u32[]{:S(2)}, u32[]{:S(2)}) %collective-permute-start.13) | collective-permute-done | bytes 319520 | tf_op jit(solution)/shard_map/ppermute | solution.py:34
  60.7 3.3 %collective-permute-start.17 = (bf16[128,768]{1,0:T(8,128)(2,1)S(1)}, bf16[128,768]{1,0:T(8,128)(2,1)S(1)}, u32[]{:S(2)}, u32[]{:S(2)}) collective-permute-start(bf16[128,768]{1,0:T(8,128)(2,1)S(1)} %get-tuple-element.141), channel_id=1, source_target_pairs={{0,2},{1,3},{2,0},{3,1},{4,6},{5,7},{6,4},{7,5},{8,10},{9,11},{10,... | collective-permute-start | bytes 589832 | tf_op jit(solution)/shard_map/ppermute | solution.py:34
  73.4 4.8 %collective-permute-done.17.refs_2_ = bf16[128,768]{1,0:T(8,128)(2,1)S(1)} collective-permute-done((bf16[128,768]{1,0:T(8,128)(2,1)S(1)}, bf16[128,768]{1,0:T(8,128)(2,1)S(1)}, u32[]{:S(2)}, u32[]{:S(2)}) %collective-permute-start.17) | collective-permute-done | bytes 196640 | tf_op jit(solution)/shard_map/ppermute | solution.py:34
  83.2 7.4 %project.1 = (bf16[512,768]{1,0:T(8,128)(2,1)}, bf16[512,2304]{1,0:T(8,128)(2,1)}, bf16[512,1536]{1,0:T(8,128)(2,1)}) custom-call(s32[8]{0:T(128)} %stack.122.table, bf16[128,768]{1,0:T(8,128)(2,1)} %get-tuple-element.152.refs_0_, bf16[128,768]{1,0:T(8,128)(2,1)} %copy-done.26, bf16[128,768]{1,0:T(8,128)(2,1)} %copy-done.27, bf16[128,768]{1,0:T(8,128)(2,1)} %copy-done.28, ...), custom_call_target="tpu_custom_call" | custom-call | flops 2310000128 | bytes 210000 | tf_op jit(solution)/shard_map/project/pallas_call | solution.py:296
  90.7 10.5 %collective-permute-done.20.refs_6_.refs_22_ = bf16[104,6144]{1,0:T(8,128)(2,1)} collective-permute-done((bf16[104,6144]{1,0:T(8,128)(2,1)}, bf16[104,6144]{1,0:T(8,128)(2,1)}, u32[]{:S(2)}, u32[]{:S(2)}) %collective-permute-start.20) | collective-permute-done | bytes 1277984 | tf_op jit(solution)/shard_map/ppermute | solution.py:39
  106.2 14.6 %attend.1 = (bf16[512,768]{1,0:T(8,128)(2,1)}, f32[512,768]{1,0:T(8,128)}) custom-call(bf16[512,2304]{1,0:T(8,128)(2,1)} %get-tuple-element.165.q_ref.k_ref.v_ref, bf16[512,2304]{1,0:T(8,128)(2,1)} %get-tuple-element.165.q_ref.k_ref.v_ref, bf16[512,2304]{1,0:T(8,128)(2,1)} %get-tuple-element.165.q_ref.k_ref.v_ref, bf16[512,1536]{1,0:T(8,128)(2,1)} %copy-done, ...), custom_call_target="tpu_custom_call" | custom-call | flops 4950000128 | bytes 450000 | tf_op jit(solution)/shard_map/attend/pallas_call | solution.py:342
  122.1 3.0 collective-permute-done.29.refs_11_.refs_27_
  126.1 33.0 %feed.1 = (f32[8,3840]{1,0:T(8,128)}, bf16[128,768]{1,0:T(8,128)(2,1)}, bf16[128,768]{1,0:T(8,128)(2,1)}, bf16[128,768]{1,0:T(8,128)(2,1)}, bf16[128,768]{1,0:T(...) custom-call(s32[8]{0:T(128)} %stack.122.table, ...), custom_call_target="tpu_custom_call" | custom-call | flops 10890000384 | bytes 990000 | tf_op jit(solution)/shard_map/feed/pallas_call | solution.py:296
  161.9 10.3 %attend_back.2 = (bf16[512,384]{1,0:T(8,128)(2,1)}, f32[512,768]{1,0:T(8,128)}, bf16[512,768]{1,0:T(8,128)(2,1)}) custom-call(bf16[512,2304]{1,0:T(8,128)(2,1)} %get-tuple-element.165.q_ref.k_ref.v_ref, bf16[512,2304]{1,0:T(8,128)(2,1)} %get-tuple-element.165.q_ref.k_ref.v_ref, bf16[512,2304]{1,0:T(8,128)(2,1)} %get-tuple-element.165.q_ref.k_ref.v_ref, ...), custom_call_target="tpu_custom_call" | custom-call | flops 2969999872 | bytes 270000 | tf_op jit(solution)/shard_map/attend_back/pallas_call | solution.py:405
  182.7 10.4 %attend_back.3 = (bf16[512,384]{1,0:T(8,128)(2,1)}, f32[512,768]{1,0:T(8,128)}, bf16[512,768]{1,0:T(8,128)(2,1)}) custom-call(bf16[512,2304]{1,0:T(8,128)(2,1)} %get-tuple-element.165.q_ref.k_ref.v_ref, bf16[512,2304]{1,0:T(8,128)(2,1)} %get-tuple-element.165.q_ref.k_ref.v_ref, bf16[512,2304]{1,0:T(8,128)(2,1)} %get-tuple-element.165.q_ref.k_ref.v_ref, ...), custom_call_target="tpu_custom_call" | custom-call | flops 2969999872 | bytes 270000 | tf_op jit(solution)/shard_map/attend_back/pallas_call | solution.py:405
  195.9 9.4 %project_back.1 = (bf16[128,768]{1,0:T(8,128)(2,1)}, bf16[128,768]{1,0:T(8,128)(2,1)}, bf16[128,768]{1,0:T(8,128)(2,1)}, bf16[128,768]{1,0:T(8,128)(2,1)}, bf16[512,2304]{1,0:T(8,128)(2,1)}) custom-call(s32[8]{0:T(128)} %stack.122.table, f32[512,768]{1,0:T(8,128)} %get-tuple-element.185.da_ref, bf16[512,384]{1,0:T(8,128)(2,1)} %get-tuple-element.188.refs_0_, ...), custom_call_target="tpu_custom_call" | custom-call | flops 2969999872 | bytes 270000 | tf_op jit(solution)/shard_map/project_back/pallas_call | solution.py:296
  205.3 6.8 %collective-permute-done.37 = bf16[2,96,3072]{2,1,0:T(8,128)(2,1)} collective-permute-done((bf16[2,96,3072]{2,1,0:T(8,128)(2,1)}, bf16[2,96,3072]{2,1,0:T(8,128)(2,1)}, u32[]{:S(2)}, u32[]{:S(2)}) %collective-permute-start.37) | collective-permute-done | bytes 1179680 | tf_op jit(solution)/shard_map/ppermute | solution.py:39
  223.6 6.8 %project_grads.1 = (f32[8,2304]{1,0:T(8,128)}, bf16[4,104,2304]{2,1,0:T(8,128)(2,1)}, bf16[4,104,2304]{2,1,0:T(8,128)(2,1)}) custom-call(s32[8]{0:T(128)} %stack.122.table, bf16[512,768]{1,0:T(8,128)(2,1)} %get-tuple-element.164.x_ref, bf16[512,2304]{1,0:T(8,128)(2,1)} %get-tuple-element.216.dqkv_ref), custom_call_target="tpu_custom_call" | custom-call | flops 2310000128 | bytes 210000 | tf_op jit(solution)/shard_map/project_grads/pallas_call | solution.py:296
  230.5 5.2 %collective-permute-done.42 = bf16[128,768]{1,0:T(8,128)(2,1)} collective-permute-done((bf16[128,768]{1,0:T(8,128)(2,1)S(1)}, bf16[128,768]{1,0:T(8,128)(2,1)}, u32[]{:S(2)}, u32[]{:S(2)}) %collective-permute-start.42) | collective-permute-done | bytes 196640 | tf_op jit(solution)/shard_map/ppermute | solution.py:34
  254.5 3.4 %collective-permute-done.46 = bf16[96,768]{1,0:T(8,128)(2,1)S(1)} collective-permute-done((bf16[96,768]{1,0:T(8,128)(2,1)S(1)}, bf16[96,768]{1,0:T(8,128)(2,1)S(1)}, u32[]{:S(2)}, u32[]{:S(2)}) %collective-permute-start.46) | collective-permute-done | bytes 147488 | tf_op jit(solution)/shard_map/ppermute | solution.py:34
  257.9 5.3 %collective-permute-done.47 = bf16[96,768]{1,0:T(8,128)(2,1)S(1)} collective-permute-done((bf16[96,768]{1,0:T(8,128)(2,1)S(1)}, bf16[96,768]{1,0:T(8,128)(2,1)S(1)}, u32[]{:S(2)}, u32[]{:S(2)}) %collective-permute-start.47) | collective-permute-done | bytes 147488 | tf_op jit(solution)/shard_map/ppermute | solution.py:34
  271.8 11.9 %collective-permute-done.51 = bf16[104,960]{1,0:T(8,128)(2,1)S(1)} collective-permute-done((bf16[104,960]{1,0:T(8,128)(2,1)S(1)}, bf16[104,960]{1,0:T(8,128)(2,1)S(1)}, u32[]{:S(2)}, u32[]{:S(2)}) %collective-permute-start.51) | collective-permute-done | bytes 199712 | tf_op jit(solution)/shard_map/ppermute | solution.py:34
  288.1 4.1 %collective-permute-start.56 = (bf16[104,576]{1,0:T(8,128)(2,1)S(1)}, bf16[104,576]{1,0:T(8,128)(2,1)S(1)}, u32[]{:S(2)}, u32[]{:S(2)}) collective-permute-start(bf16[104,576]{1,0:T(8,128)(2,1)S(1)} %pad_maximum_fusion.12), channel_id=1, source_target_pairs={{0,2},{1,3},{2,0},{3,1},{4,6},{5,7},{6,4},{7,5},{8,10},{9,11},{10,... | collective-permute-start | bytes 359432 | tf_op jit(solution)/shard_map/ppermute | solution.py:34
  295.8 5.0 %collective-permute-done.56 = bf16[104,576]{1,0:T(8,128)(2,1)S(1)} collective-permute-done((bf16[104,576]{1,0:T(8,128)(2,1)S(1)}, bf16[104,576]{1,0:T(8,128)(2,1)S(1)}, u32[]{:S(2)}, u32[]{:S(2)}) %collective-permute-start.56) | collective-permute-done | bytes 119840 | tf_op jit(solution)/shard_map/ppermute | solution.py:34
  (272 shorter events, 110.3 us)
Async XLA Ops:
  24.0 31.7 %collective-permute-start.8 = (bf16[104,3072]{1,0:T(8,128)(2,1)S(1)}, bf16[104,3072]{1,0:T(8,128)(2,1)}, u32[]{:S(2)}, u32[]{:S(2)}) collective-permute-start(bf16[104,3072]{1,0:T(8,128)(2,1)S(1)} %maximum_maximum_fusion.refs_5_.refs_12_.refs_6_), channel_id=1, source_target_pairs={{0,24},{4,28},{8,16},{12,20},{16,8},{20,12},{24,0},{28,4},{1,25},{... | collective-permute-start | bytes 1916936 | tf_op jit(solution)/shard_map/ppermute | solution.py:39
  26.5 29.7 %collective-permute-start.7 = (bf16[104,3072]{1,0:T(8,128)(2,1)S(1)}, bf16[104,3072]{1,0:T(8,128)(2,1)}, u32[]{:S(2)}, u32[]{:S(2)}) collective-permute-start(bf16[104,3072]{1,0:T(8,128)(2,1)S(1)} %maximum_maximum_fusion.refs_5_.refs_12_.refs_6_), channel_id=1, source_target_pairs={{0,16},{4,12},{8,24},{12,4},{16,0},{20,28},{24,8},{28,20},{1,17},{... | collective-permute-start | bytes 1916936 | tf_op jit(solution)/shard_map/ppermute | solution.py:39
  27.0 29.2 %collective-permute-start.6 = (bf16[104,3072]{1,0:T(8,128)(2,1)S(1)}, bf16[104,3072]{1,0:T(8,128)(2,1)}, u32[]{:S(2)}, u32[]{:S(2)}) collective-permute-start(bf16[104,3072]{1,0:T(8,128)(2,1)S(1)} %maximum_maximum_fusion.refs_5_.refs_12_.refs_6_), channel_id=1, source_target_pairs={{0,8},{4,20},{8,0},{12,28},{16,24},{20,4},{24,16},{28,12},{1,9},{5... | collective-permute-start | bytes 1916936 | tf_op jit(solution)/shard_map/ppermute | solution.py:39
  30.6 25.0 %collective-permute-start.14 = (bf16[104,1536]{1,0:T(8,128)(2,1)S(1)}, bf16[104,1536]{1,0:T(8,128)(2,1)S(1)}, u32[]{:S(2)}, u32[]{:S(2)}) collective-permute-start(bf16[104,1536]{1,0:T(8,128)(2,1)S(1)} %pad_maximum_fusion.5), channel_id=1, source_target_pairs={{0,2},{1,3},{2,0},{3,1},{4,6},{5,7},{6,4},{7,5},{8,10},{9,11},{10,... | collective-permute-start | bytes 958472 | tf_op jit(solution)/shard_map/ppermute | solution.py:34
  40.5 20.0 %collective-permute-start.13 = (bf16[104,1536]{1,0:T(8,128)(2,1)S(1)}, bf16[104,1536]{1,0:T(8,128)(2,1)S(1)}, u32[]{:S(2)}, u32[]{:S(2)}) collective-permute-start(bf16[104,1536]{1,0:T(8,128)(2,1)S(1)} %pad_maximum_fusion.5), channel_id=1, source_target_pairs={{0,1},{1,0},{2,3},{3,2},{4,5},{5,4},{6,7},{7,6},{8,9},{9,8},{10,11... | collective-permute-start | bytes 958472 | tf_op jit(solution)/shard_map/ppermute | solution.py:34
  60.7 17.6 %collective-permute-start.17 = (bf16[128,768]{1,0:T(8,128)(2,1)S(1)}, bf16[128,768]{1,0:T(8,128)(2,1)S(1)}, u32[]{:S(2)}, u32[]{:S(2)}) collective-permute-start(bf16[128,768]{1,0:T(8,128)(2,1)S(1)} %get-tuple-element.141), channel_id=1, source_target_pairs={{0,2},{1,3},{2,0},{3,1},{4,6},{5,7},{6,4},{7,5},{8,10},{9,11},{10,... | collective-permute-start | bytes 589832 | tf_op jit(solution)/shard_map/ppermute | solution.py:34
  70.5 30.6 %collective-permute-start.20 = (bf16[104,6144]{1,0:T(8,128)(2,1)}, bf16[104,6144]{1,0:T(8,128)(2,1)}, u32[]{:S(2)}, u32[]{:S(2)}) collective-permute-start(bf16[104,6144]{1,0:T(8,128)(2,1)} %constant_dynamic-update-slice_fusion.refs_4_.refs_20_), channel_id=1, source_target_pairs={{0,16},{4,12},{8,24},{12,4},{16,0},{20,28},{24,8},{28,20},{1,17},{... | collective-permute-start | bytes 3833864 | tf_op jit(solution)/shard_map/ppermute | solution.py:39
  71.9 29.3 %collective-permute-start.19 = (bf16[104,6144]{1,0:T(8,128)(2,1)}, bf16[104,6144]{1,0:T(8,128)(2,1)}, u32[]{:S(2)}, u32[]{:S(2)}) collective-permute-start(bf16[104,6144]{1,0:T(8,128)(2,1)} %constant_dynamic-update-slice_fusion.refs_4_.refs_20_), channel_id=1, source_target_pairs={{0,8},{4,20},{8,0},{12,28},{16,24},{20,4},{24,16},{28,12},{1,9},{5... | collective-permute-start | bytes 3833864 | tf_op jit(solution)/shard_map/ppermute | solution.py:39
  78.2 23.0 %collective-permute-start.22 = (bf16[104,6144]{1,0:T(8,128)(2,1)}, bf16[104,6144]{1,0:T(8,128)(2,1)}, u32[]{:S(2)}, u32[]{:S(2)}) collective-permute-start(bf16[104,6144]{1,0:T(8,128)(2,1)} %constant_dynamic-update-slice_fusion.refs_4_.refs_20_), channel_id=1, source_target_pairs={{0,4},{4,0},{8,12},{12,8},{16,20},{20,16},{24,28},{28,24},{1,5},{5... | collective-permute-start | bytes 3833864 | tf_op jit(solution)/shard_map/ppermute | solution.py:39
  101.2 19.7 %collective-permute-start.26 = (bf16[104,6144]{1,0:T(8,128)(2,1)}, bf16[104,6144]{1,0:T(8,128)(2,1)S(1)}, u32[]{:S(2)}, u32[]{:S(2)}) collective-permute-start(bf16[104,6144]{1,0:T(8,128)(2,1)} %collective-permute-done.20.refs_6_.refs_22_), channel_id=1, source_target_pairs={{0,4},{4,0},{8,12},{12,8},{16,20},{20,16},{24,28},{28,24},{1,5},{5... | collective-permute-start | bytes 3833864 | tf_op jit(solution)/shard_map/ppermute | solution.py:39
  101.7 19.2 %collective-permute-start.25 = (bf16[104,6144]{1,0:T(8,128)(2,1)}, bf16[104,6144]{1,0:T(8,128)(2,1)S(1)}, u32[]{:S(2)}, u32[]{:S(2)}) collective-permute-start(bf16[104,6144]{1,0:T(8,128)(2,1)} %collective-permute-done.19.refs_5_.refs_21_), channel_id=1, source_target_pairs={{0,4},{4,0},{8,12},{12,8},{16,20},{20,16},{24,28},{28,24},{1,5},{5... | collective-permute-start | bytes 3833864 | tf_op jit(solution)/shard_map/ppermute | solution.py:39
  101.8 19.2 %collective-permute-start.24 = (bf16[104,6144]{1,0:T(8,128)(2,1)}, bf16[104,6144]{1,0:T(8,128)(2,1)S(1)}, u32[]{:S(2)}, u32[]{:S(2)}) collective-permute-start(bf16[104,6144]{1,0:T(8,128)(2,1)} %collective-permute-done.19.refs_5_.refs_21_), channel_id=1, source_target_pairs={{0,16},{4,12},{8,24},{12,4},{16,0},{20,28},{24,8},{28,20},{1,17},{... | collective-permute-start | bytes 3833864 | tf_op jit(solution)/shard_map/ppermute | solution.py:39
  103.3 17.6 %collective-permute-start.28 = (bf16[128,768]{1,0:T(8,128)(2,1)S(1)}, bf16[128,768]{1,0:T(8,128)(2,1)S(1)}, u32[]{:S(2)}, u32[]{:S(2)}) collective-permute-start(bf16[128,768]{1,0:T(8,128)(2,1)S(1)} %get-tuple-element.292), channel_id=1, source_target_pairs={{0,2},{1,3},{2,0},{3,1},{4,6},{5,7},{6,4},{7,5},{8,10},{9,11},{10,... | collective-permute-start | bytes 589832 | tf_op jit(solution)/shard_map/ppermute | solution.py:34
  104.8 16.1 %collective-permute-start.27 = (bf16[128,768]{1,0:T(8,128)(2,1)S(1)}, bf16[128,768]{1,0:T(8,128)(2,1)S(1)}, u32[]{:S(2)}, u32[]{:S(2)}) collective-permute-start(bf16[128,768]{1,0:T(8,128)(2,1)S(1)} %get-tuple-element.293), channel_id=1, source_target_pairs={{0,1},{1,0},{2,3},{3,2},{4,5},{5,4},{6,7},{7,6},{8,9},{9,8},{10,11... | collective-permute-start | bytes 589832 | tf_op jit(solution)/shard_map/ppermute | solution.py:34
  172.2 20.9 %collective-permute-start.33 = (bf16[512,768]{1,0:T(8,128)(2,1)}, bf16[512,768]{1,0:T(8,128)(2,1)}, u32[]{:S(2)}, u32[]{:S(2)}) collective-permute-start(bf16[512,768]{1,0:T(8,128)(2,1)} %get-tuple-element.201), channel_id=1, source_target_pairs={{0,4},{4,0},{8,12},{12,8},{16,20},{20,16},{24,28},{28,24},{1,5},{5... | collective-permute-start | bytes 2359304 | tf_op jit(solution)/shard_map/ppermute | solution.py:39
  178.4 33.6 %collective-permute-start.38 = (bf16[2,104,3840]{2,1,0:T(8,128)(2,1)}, bf16[2,104,3840]{2,1,0:T(8,128)(2,1)}, u32[]{:S(2)}, u32[]{:S(2)}) collective-permute-start(bf16[2,104,3840]{2,1,0:T(8,128)(2,1)} %add_convert_fusion), channel_id=1, source_target_pairs={{0,16},{4,12},{8,24},{12,4},{16,0},{20,28},{24,8},{28,20},{1,17},{... | collective-permute-start | bytes 4792328 | tf_op jit(solution)/shard_map/ppermute | solution.py:39
  182.0 30.1 %collective-permute-start.37 = (bf16[2,96,3072]{2,1,0:T(8,128)(2,1)}, bf16[2,96,3072]{2,1,0:T(8,128)(2,1)}, u32[]{:S(2)}, u32[]{:S(2)}) collective-permute-start(bf16[2,96,3072]{2,1,0:T(8,128)(2,1)} %add_convert_fusion.1), channel_id=1, source_target_pairs={{0,16},{4,12},{8,24},{12,4},{16,0},{20,28},{24,8},{28,20},{1,17},{... | collective-permute-start | bytes 3538952 | tf_op jit(solution)/shard_map/ppermute | solution.py:39
  217.2 18.8 %collective-permute-start.40 = (bf16[1,104,3840]{2,1,0:T(8,128)(2,1)}, bf16[1,104,3840]{2,1,0:T(8,128)(2,1)}, u32[]{:S(2)}, u32[]{:S(2)}) collective-permute-start(bf16[1,104,3840]{2,1,0:T(8,128)(2,1)} %add_convert_fusion.3), channel_id=1, source_target_pairs={{0,8},{4,20},{8,0},{12,28},{16,24},{20,4},{24,16},{28,12},{1,9},{5... | collective-permute-start | bytes 2396168 | tf_op jit(solution)/shard_map/ppermute | solution.py:39
  217.6 18.3 %collective-permute-start.39 = (bf16[1,96,3072]{2,1,0:T(8,128)(2,1)}, bf16[1,96,3072]{2,1,0:T(8,128)(2,1)}, u32[]{:S(2)}, u32[]{:S(2)}) collective-permute-start(bf16[1,96,3072]{2,1,0:T(8,128)(2,1)} %add_convert_fusion.4), channel_id=1, source_target_pairs={{0,8},{4,20},{8,0},{12,28},{16,24},{20,4},{24,16},{28,12},{1,9},{5... | collective-permute-start | bytes 1769480 | tf_op jit(solution)/shard_map/ppermute | solution.py:39
  219.3 16.4 %collective-permute-start.42 = (bf16[128,768]{1,0:T(8,128)(2,1)S(1)}, bf16[128,768]{1,0:T(8,128)(2,1)}, u32[]{:S(2)}, u32[]{:S(2)}) collective-permute-start(bf16[128,768]{1,0:T(8,128)(2,1)S(1)} %copy-done.32), channel_id=1, source_target_pairs={{0,2},{1,3},{2,0},{3,1},{4,6},{5,7},{6,4},{7,5},{8,10},{9,11},{10,... | collective-permute-start | bytes 589832 | tf_op jit(solution)/shard_map/ppermute | solution.py:34
  244.4 18.9 %collective-permute-start.45 = (bf16[2,104,2304]{2,1,0:T(8,128)(2,1)S(1)}, bf16[2,104,2304]{2,1,0:T(8,128)(2,1)S(1)}, u32[]{:S(2)}, u32[]{:S(2)}) collective-permute-start(bf16[2,104,2304]{2,1,0:T(8,128)(2,1)S(1)} %add_convert_fusion.2), channel_id=1, source_target_pairs={{0,16},{4,12},{8,24},{12,4},{16,0},{20,28},{24,8},{28,20},{1,17},{... | collective-permute-start | bytes 2875400 | tf_op jit(solution)/shard_map/ppermute | solution.py:39
  253.4 18.4 %collective-permute-start.50 = (bf16[104,960]{1,0:T(8,128)(2,1)S(1)}, bf16[104,960]{1,0:T(8,128)(2,1)S(1)}, u32[]{:S(2)}, u32[]{:S(2)}) collective-permute-start(bf16[104,960]{1,0:T(8,128)(2,1)S(1)} %pad_maximum_fusion.7), channel_id=1, source_target_pairs={{0,1},{1,0},{2,3},{3,2},{4,5},{5,4},{6,7},{7,6},{8,9},{9,8},{10,11... | collective-permute-start | bytes 599048 | tf_op jit(solution)/shard_map/ppermute | solution.py:34
  264.5 19.2 %collective-permute-start.49 = (bf16[1,104,2304]{2,1,0:T(8,128)(2,1)S(1)}, bf16[1,104,2304]{2,1,0:T(8,128)(2,1)S(1)}, u32[]{:S(2)}, u32[]{:S(2)}) collective-permute-start(bf16[1,104,2304]{2,1,0:T(8,128)(2,1)S(1)} %add_convert_fusion.5), channel_id=1, source_target_pairs={{0,8},{4,20},{8,0},{12,28},{16,24},{20,4},{24,16},{28,12},{1,9},{5... | collective-permute-start | bytes 1437704 | tf_op jit(solution)/shard_map/ppermute | solution.py:39
  266.1 17.6 %collective-permute-start.51 = (bf16[104,960]{1,0:T(8,128)(2,1)S(1)}, bf16[104,960]{1,0:T(8,128)(2,1)S(1)}, u32[]{:S(2)}, u32[]{:S(2)}) collective-permute-start(bf16[104,960]{1,0:T(8,128)(2,1)S(1)} %pad_maximum_fusion.8), channel_id=1, source_target_pairs={{0,2},{1,3},{2,0},{3,1},{4,6},{5,7},{6,4},{7,5},{8,10},{9,11},{10,... | collective-permute-start | bytes 599048 | tf_op jit(solution)/shard_map/ppermute | solution.py:34
  (71 other events, 695.3 us)
